TPU v7x, 32 devices: a whole 2x2x4 slice. The times are simulated.
32 devices in a mesh: pb: 8 (over z, x), ka: 4 (over y, core).
Axes of the slice: x: 2, y: 2, z: 4, core: 2. Of those that a mesh axis runs over, the one named last changes fastest.
Arguments:
- queries: bfloat16 [4096, 128], P('pb'), may hold values from -96 to 96
- keys: bfloat16 [32768, 128], P('ka'), may hold values from -4 to 4
- values: bfloat16 [32768, 128], P('ka'), may hold values from -6 to 6
- bias: float32 [32768], P(('pb', 'ka')), may hold values from -6 to 6
- grad_out: bfloat16 [4096, 128], P('pb'), may hold values from -1536 to 1536
- group_start: int32 [1], replicated, may hold values from 8192 to 28672
Outputs:
- query_grad: bfloat16 [4096, 128], P(('pb', 'ka'))
- key_grad: bfloat16 [32768, 128], P(('ka', 'pb'))
- value_grad: bfloat16 [32768, 128], P(('ka', 'pb'))
- bias_grad: float32 [32768], P(('pb', 'ka'))
All inputs are finite; a program needn't handle non-finite values.
Results may differ from a plain program's by a relative error of at most 0.015.
Values may be sent and summed in bfloat16 or wider, within the bound.
A program may use at most 128 MiB of HBM per device.

v0:
```python
import jax
import jax.numpy as jnp
from jax import lax
from jax.sharding import PartitionSpec as P

negative = -1e30


def combined_all(x, axis, combine):
    everything = jax.tree.map(lambda part: lax.all_gather(part, axis), x)
    initial = jax.tree.map(lambda part: part[0], everything)

    def turn(k, so_far):
        return combine(so_far, jax.tree.map(lambda part: part[k], everything))

    return lax.fori_loop(1, lax.axis_size(axis), turn, initial)


def toeplitz_rows(segment, row_count, col_count):
    length = row_count + col_count - 1
    backward = segment[::-1]
    tiled = jnp.tile(backward, row_count + 1)[: row_count * (length + 1)].reshape(
        row_count, length + 1
    )
    return tiled[::-1, :col_count]


def diagonal_sums(dscore_mat, row_count, col_count):
    length = row_count + col_count - 1
    flipped = dscore_mat[:, ::-1]
    padded = jnp.pad(flipped, ((0, 0), (0, row_count)))
    skewed = padded.reshape(-1)[: row_count * length].reshape(row_count, length)
    return jnp.sum(skewed, axis=0)


def combine(first_part, second_part):
    row_max = jnp.maximum(first_part[0], second_part[0])
    first_scale = jnp.exp(first_part[0] - row_max)
    second_scale = jnp.exp(second_part[0] - row_max)
    row_sum = first_part[1] * first_scale + second_part[1] * second_scale
    weighted = first_part[2] * first_scale[:, None] + second_part[2] * second_scale[:, None]
    return (row_max, row_sum, weighted)


def block_scores(query_block, key_block, first_query, first_key, bias_padded, margin, score_scale):
    row_count = query_block.shape[0]
    col_count = key_block.shape[0]
    diag_start = first_query - first_key - (col_count - 1)
    segment = lax.dynamic_slice_in_dim(bias_padded, diag_start + margin, row_count + col_count - 1)
    row_ids = lax.broadcasted_iota(jnp.int32, (row_count, col_count), 0)
    col_ids = lax.broadcasted_iota(jnp.int32, (row_count, col_count), 1)
    visible = first_query - first_key + row_ids - col_ids >= 0
    scores = (
        jnp.einsum("qd,kd->qk", query_block, key_block, preferred_element_type=jnp.float32)
        * score_scale
    )
    scores = scores + toeplitz_rows(segment, row_count, col_count)
    return (scores, visible)


def forward_block(
    query_block, key_block, value_block, first_query, first_key, bias_padded, margin, score_scale
):
    scores, visible = block_scores(
        query_block, key_block, first_query, first_key, bias_padded, margin, score_scale
    )
    row_max = jnp.max(jnp.where(visible, scores, negative), axis=1)
    weights = jnp.where(visible, jnp.exp(scores - row_max[:, None]), 0.0)
    row_sum = jnp.sum(weights, axis=1)
    weighted = jnp.dot(
        weights.astype(jnp.bfloat16), value_block, preferred_element_type=jnp.float32
    )
    return (row_max, row_sum, weighted)


def backward_block(
    query_block,
    grad_block,
    log_norm,
    row_dots,
    key_block,
    value_block,
    first_query,
    first_key,
    bias_padded,
    margin,
    score_scale,
):
    row_count = query_block.shape[0]
    col_count = key_block.shape[0]
    diag_start = first_query - first_key - (col_count - 1)
    scores, visible = block_scores(
        query_block, key_block, first_query, first_key, bias_padded, margin, score_scale
    )
    prob_mat = jnp.where(visible, jnp.exp(scores - log_norm[:, None]), 0.0)
    dprob_mat = jnp.einsum("qd,kd->qk", grad_block, value_block, preferred_element_type=jnp.float32)
    dscore_mat = prob_mat * (dprob_mat - row_dots[:, None])
    dscore_low = dscore_mat.astype(jnp.bfloat16)
    query_part = jnp.dot(dscore_low, key_block, preferred_element_type=jnp.float32)
    key_part = jnp.einsum("qk,qd->kd", dscore_low, query_block, preferred_element_type=jnp.float32)
    value_part = jnp.einsum(
        "qk,qd->kd", prob_mat.astype(jnp.bfloat16), grad_block, preferred_element_type=jnp.float32
    )
    query_part, key_part, value_part, diag_part = (
        query_part,
        key_part,
        value_part,
        diagonal_sums(dscore_mat, row_count, col_count),
    )
    return (query_part, key_part, value_part, diag_part, diag_start)


def add_diagonals(offset_acc, diag_part, diag_start, margin):
    place_at = diag_start + margin
    old_values = lax.dynamic_slice_in_dim(offset_acc, place_at, diag_part.shape[0])
    return lax.dynamic_update_slice_in_dim(offset_acc, old_values + diag_part, place_at, 0)


def on_device(queries, keys, values, bias, grad_out, group_start):
    head_dim = queries.shape[1]
    score_scale = head_dim ** (-0.5)
    group_first = group_start[0]
    key_count = keys.shape[0]
    row_count = queries.shape[0]
    key_base = lax.axis_index("ka") * key_count
    first_query = group_first + lax.axis_index("pb") * row_count
    bias_whole = lax.all_gather(bias, ("pb", "ka"), axis=0, tiled=True)
    offset_count = bias_whole.shape[0]
    margin = max(row_count, min(512, row_count * lax.axis_size("pb"))) + key_count
    bias_padded = jnp.pad(bias_whole, (margin, margin))
    block_size = min(2048, key_count)
    block_count = key_count // block_size
    key_parts = keys.reshape(block_count, block_size, head_dim)
    value_parts = values.reshape(block_count, block_size, head_dim)
    block_ids = jnp.arange(block_count, dtype=jnp.int32)

    def forward_step(running, pieces):
        key_block, value_block, block_id = pieces
        stats = forward_block(
            queries,
            key_block,
            value_block,
            first_query,
            key_base + block_id * block_size,
            bias_padded,
            margin,
            score_scale,
        )
        return (combine(running, stats), None)

    start_stats = (
        jnp.full((row_count,), negative, jnp.float32),
        jnp.zeros((row_count,), jnp.float32),
        jnp.zeros((row_count, head_dim), jnp.float32),
    )
    local_stats, unused = lax.scan(forward_step, start_stats, (key_parts, value_parts, block_ids))
    row_max, row_sum, weighted = combined_all(
        (local_stats[0], local_stats[1], local_stats[2]), "ka", combine
    )
    log_norm = row_max + jnp.log(row_sum)
    row_dots = jnp.sum(grad_out.astype(jnp.float32) * (weighted / row_sum[:, None]), axis=1)
    group_queries, group_grads = (
        lax.all_gather(queries, "pb", axis=0, tiled=True),
        lax.all_gather(grad_out, "pb", axis=0, tiled=True),
    )
    group_norm, group_dots = (
        lax.all_gather(log_norm, "pb", axis=0, tiled=True),
        lax.all_gather(row_dots, "pb", axis=0, tiled=True),
    )
    own_count = key_count // lax.axis_size("pb")
    own_start = lax.axis_index("pb") * own_count
    own_keys = lax.dynamic_slice_in_dim(keys, own_start, own_count, 0)
    own_values = lax.dynamic_slice_in_dim(values, own_start, own_count, 0)
    first_key = key_base + own_start
    total_rows = group_queries.shape[0]
    query_size = min(512, total_rows)
    query_count = total_rows // query_size
    query_parts = group_queries.reshape(query_count, query_size, head_dim)
    grad_parts = group_grads.reshape(query_count, query_size, head_dim)
    norm_parts = group_norm.reshape(query_count, query_size)
    dots_parts = group_dots.reshape(query_count, query_size)
    query_ids = jnp.arange(query_count, dtype=jnp.int32)

    def backward_step(running, pieces):
        key_acc, value_acc, offset_acc = running
        query_block, grad_block, norm_block, dots_block, block_id = pieces
        query_part, key_part, value_part, diag_part, diag_start = backward_block(
            query_block,
            grad_block,
            norm_block,
            dots_block,
            own_keys,
            own_values,
            group_first + block_id * query_size,
            first_key,
            bias_padded,
            margin,
            score_scale,
        )
        return (
            (
                key_acc + key_part,
                value_acc + value_part,
                add_diagonals(offset_acc, diag_part, diag_start, margin),
            ),
            query_part,
        )

    start_back = (
        jnp.zeros((own_count, head_dim), jnp.float32),
        jnp.zeros((own_count, head_dim), jnp.float32),
        jnp.zeros(bias_padded.shape, jnp.float32),
    )
    final_back, query_pieces = lax.scan(
        backward_step, start_back, (query_parts, grad_parts, norm_parts, dots_parts, query_ids)
    )
    key_sum, value_sum, offset_acc = final_back
    query_sum = lax.psum_scatter(
        query_pieces.reshape(total_rows, head_dim), ("pb", "ka"), scatter_dimension=0, tiled=True
    )
    bias_grad = lax.psum_scatter(
        offset_acc[margin : margin + offset_count], ("pb", "ka"), scatter_dimension=0, tiled=True
    )
    query_grad = (query_sum * score_scale).astype(jnp.bfloat16)
    key_grad = (key_sum * score_scale).astype(jnp.bfloat16)
    value_grad = value_sum.astype(jnp.bfloat16)
    return (query_grad, key_grad, value_grad, bias_grad)


def solution(mesh):
    return jax.shard_map(
        on_device,
        mesh=mesh,
        in_specs=(P("pb", None), P("ka", None), P("ka", None), P(("pb", "ka")), P("pb", None), P()),
        out_specs=(
            P(("pb", "ka"), None),
            P(("ka", "pb"), None),
            P(("ka", "pb"), None),
            P(("pb", "ka")),
        ),
        check_vma=False,
    )
```

profile of v0, /device:TPU:0, one launch (start us, length us, event | category | flops | bytes accessed | tf_op | source)
XLA Modules:
  0.0 1173.5 jit_solution(6646514406511590905)
XLA Ops:
  7.9 43.9 %all_gather.34 = f32[32768]{0:T(1024)S(1)} all-gather(f32[1024]{0:T(1024)} %param.15), channel_id=1, replica_groups=mesh['pb'=8,'ka'=4] {'pb','ka'}, dimensions={0}, use_global_device_ids=true | all-gather | bytes 135168 | tf_op jit(solution)/shard_map/all_gather | solution.py:127
  51.8 299.9 %while.60 = (s32[]{:T(128)}, f32[512]{0:T(512)S(1)}, f32[512]{0:T(512)S(1)}, f32[512,128]{1,0:T(8,128)S(1)}, s32[4]{0:T(128)S(1)}, /*index=5*/s32[]{:T(128)}, s3...) while((s32[]{:T(128)}, f32[512]{0:T(512)S(1)}, ...), condition=%wide.region_3.4_spmd.clone, body=%wide.region_0.3_spmd.clone.sunk | while | flops 553913856 | bytes 81004816 | solution.py:156
  56.4 8.1 tile.51
  64.4 4.3 slice.88
  68.7 6.7 reshape.119
  75.4 4.7 slice.89
  80.1 5.3 copy.27
  85.5 34.4 %rev.53 = f32[512,2048]{0,1:T(8,128)} reverse(f32[512,2048]{0,1:T(8,128)} %copy.27), dimensions={0} | reverse | bytes 8388608 | tf_op jit(solution)/shard_map/while/body/eval_jaxpr/rev | solution.py:25
  131.3 8.1 tile.51
  139.4 4.3 slice.88
  143.7 6.7 reshape.119
  150.4 4.7 slice.89
  155.1 5.3 copy.27
  160.5 34.4 %rev.53 = f32[512,2048]{0,1:T(8,128)} reverse(f32[512,2048]{0,1:T(8,128)} %copy.27), dimensions={0} | reverse | bytes 8388608 | tf_op jit(solution)/shard_map/while/body/eval_jaxpr/rev | solution.py:25
  206.3 8.1 tile.51
  214.4 4.3 slice.88
  218.7 6.7 reshape.119
  225.4 4.7 slice.89
  230.1 5.3 copy.27
  235.4 34.4 %rev.53 = f32[512,2048]{0,1:T(8,128)} reverse(f32[512,2048]{0,1:T(8,128)} %copy.27), dimensions={0} | reverse | bytes 8388608 | tf_op jit(solution)/shard_map/while/body/eval_jaxpr/rev | solution.py:25
  281.3 8.1 tile.51
  289.4 4.3 slice.88
  293.6 6.7 reshape.119
  300.4 4.7 slice.89
  305.1 5.3 copy.27
  310.4 34.4 %rev.53 = f32[512,2048]{0,1:T(8,128)} reverse(f32[512,2048]{0,1:T(8,128)} %copy.27), dimensions={0} | reverse | bytes 8388608 | tf_op jit(solution)/shard_map/while/body/eval_jaxpr/rev | solution.py:25
  354.0 5.2 all-gather.3
  359.2 5.3 all-gather.4
  371.3 26.2 %all-gather.6 = f32[8,1,512]{2,1,0:T(1,128)S(1)} all-gather(f32[1,1,512]{2,1,0:T(1,128)S(1)} %bitcast.131), channel_id=1, replica_groups=mesh['pb'=8,'ka'=4] {'pb'}, dimensions={0}, use_global_device_ids=true | all-gather | bytes 18432 | tf_op jit(solution)/shard_map/all_gather | solution.py:168
  397.6 26.3 %all-gather.5 = f32[8,1,512]{2,1,0:T(1,128)S(1)} all-gather(f32[1,1,512]{2,1,0:T(1,128)S(1)} %bitcast.132), channel_id=1, replica_groups=mesh['pb'=8,'ka'=4] {'pb'}, dimensions={0}, use_global_device_ids=true | all-gather | bytes 18432 | tf_op jit(solution)/shard_map/all_gather | solution.py:167
  423.9 25.0 %all-gather.13.cloned.1.call-done = bf16[4096,128]{1,0:T(8,128)(2,1)} async-done(((bf16[512,128]{1,0:T(8,128)(2,1)}), bf16[4096,128]{1,0:T(8,128)(2,1)}) %all-gather.13.cloned.1.call-update) | async-done | bytes 1048592 | tf_op jit(solution)/shard_map/all_gather | solution.py:164
  449.6 451.8 %while.61 = (s32[]{:T(128)}, f32[1024,128]{1,0:T(8,128)}, f32[1024,128]{1,0:T(8,128)}, f32[50176]{0:T(1024)}, f32[8,512,128]{2,1,0:T(8,128)}, /*index=5*/s32[8]{...) while((s32[]{:T(128)}, f32[1024,128]{1,0:T(8,128)}, ...), condition=%wide.region_9.10_spmd.clone, body=%wide.region_7.9_spmd.clone.sunk | while | flops 678166528 | bytes 90305048 | solution.py:214
  452.1 3.9 tile.53
  461.5 10.5 rev.54
  480.4 11.8 %rev.55 = f32[512,1024]{1,0:T(8,128)} reverse(f32[512,1024]{1,0:T(8,128)S(1)} %subtract_multiply_fusion.2), dimensions={1} | reverse | bytes 4194304 | tf_op jit(solution)/shard_map/while/body/eval_jaxpr/rev | solution.py:30
  498.6 3.8 reshape.122
  508.6 3.9 tile.53
  517.9 10.5 rev.54
  536.9 11.8 %rev.55 = f32[512,1024]{1,0:T(8,128)} reverse(f32[512,1024]{1,0:T(8,128)S(1)} %subtract_multiply_fusion.2), dimensions={1} | reverse | bytes 4194304 | tf_op jit(solution)/shard_map/while/body/eval_jaxpr/rev | solution.py:30
  555.1 3.8 reshape.122
  565.1 3.9 tile.53
  574.4 10.5 rev.54
  593.4 11.8 %rev.55 = f32[512,1024]{1,0:T(8,128)} reverse(f32[512,1024]{1,0:T(8,128)S(1)} %subtract_multiply_fusion.2), dimensions={1} | reverse | bytes 4194304 | tf_op jit(solution)/shard_map/while/body/eval_jaxpr/rev | solution.py:30
  611.5 3.8 reshape.122
  621.5 3.9 tile.53
  630.9 10.5 rev.54
  649.8 11.8 %rev.55 = f32[512,1024]{1,0:T(8,128)} reverse(f32[512,1024]{1,0:T(8,128)S(1)} %subtract_multiply_fusion.2), dimensions={1} | reverse | bytes 4194304 | tf_op jit(solution)/shard_map/while/body/eval_jaxpr/rev | solution.py:30
  668.0 3.8 reshape.122
  678.0 3.9 tile.53
  687.3 10.5 rev.54
  706.3 11.8 %rev.55 = f32[512,1024]{1,0:T(8,128)} reverse(f32[512,1024]{1,0:T(8,128)S(1)} %subtract_multiply_fusion.2), dimensions={1} | reverse | bytes 4194304 | tf_op jit(solution)/shard_map/while/body/eval_jaxpr/rev | solution.py:30
  734.5 3.9 tile.53
  743.8 10.5 rev.54
  762.8 11.8 %rev.55 = f32[512,1024]{1,0:T(8,128)} reverse(f32[512,1024]{1,0:T(8,128)S(1)} %subtract_multiply_fusion.2), dimensions={1} | reverse | bytes 4194304 | tf_op jit(solution)/shard_map/while/body/eval_jaxpr/rev | solution.py:30
  781.0 3.8 reshape.122
  791.0 3.9 tile.53
  800.3 10.5 rev.54
  819.3 11.8 %rev.55 = f32[512,1024]{1,0:T(8,128)} reverse(f32[512,1024]{1,0:T(8,128)S(1)} %subtract_multiply_fusion.2), dimensions={1} | reverse | bytes 4194304 | tf_op jit(solution)/shard_map/while/body/eval_jaxpr/rev | solution.py:30
  837.4 3.8 reshape.122
  847.4 3.9 tile.53
  856.8 10.5 rev.54
  875.7 11.8 %rev.55 = f32[512,1024]{1,0:T(8,128)} reverse(f32[512,1024]{1,0:T(8,128)S(1)} %subtract_multiply_fusion.2), dimensions={1} | reverse | bytes 4194304 | tf_op jit(solution)/shard_map/while/body/eval_jaxpr/rev | solution.py:30
  906.2 120.2 %all-reduce.5.cloned.1.call-done = f32[32768]{0:T(1024)} async-done(((f32[32768]{0:T(1024)}), f32[32768]{0:T(1024)}) %all-reduce.5.cloned.1.call-update) | async-done | bytes 131088
  1027.7 137.9 %reduce-scatter.2.cloned.1.call-done = f32[128,128]{1,0:T(8,128)} async-done(((f32[4096,128]{1,0:T(8,128)}), f32[128,128]{1,0:T(8,128)}) %reduce-scatter.2.cloned.1.call-update) | async-done | bytes 65552 | tf_op jit(solution)/shard_map/reduce_scatter | solution.py:218
  (383 shorter events, 272.1 us)
Async XLA Ops:
  7.2 359.2 %all-gather.15.cloned.1.call-start = ((), (), s32[]{:S(2)}) async-start(), calls=%async_computation.4 | async-start | bytes 1310720 | tf_op jit(solution)/shard_map/all_gather | solution.py:10
  85.5 34.4 %copy-start.6 = (bf16[512,128]{1,0:T(8,128)(2,1)S(1)}, bf16[512,128]{1,0:T(8,128)(2,1)}, u32[]{:S(2)}) copy-start(bf16[512,128]{1,0:T(8,128)(2,1)} %get-tuple-element.1147) | copy-start | bytes 393220 | tf_op jit(solution)/shard_map/while
  160.5 34.4 %copy-start.6 = (bf16[512,128]{1,0:T(8,128)(2,1)S(1)}, bf16[512,128]{1,0:T(8,128)(2,1)}, u32[]{:S(2)}) copy-start(bf16[512,128]{1,0:T(8,128)(2,1)} %get-tuple-element.1147) | copy-start | bytes 393220 | tf_op jit(solution)/shard_map/while
  235.4 34.4 %copy-start.6 = (bf16[512,128]{1,0:T(8,128)(2,1)S(1)}, bf16[512,128]{1,0:T(8,128)(2,1)}, u32[]{:S(2)}) copy-start(bf16[512,128]{1,0:T(8,128)(2,1)} %get-tuple-element.1147) | copy-start | bytes 393220 | tf_op jit(solution)/shard_map/while
  310.4 34.4 %copy-start.6 = (bf16[512,128]{1,0:T(8,128)(2,1)S(1)}, bf16[512,128]{1,0:T(8,128)(2,1)}, u32[]{:S(2)}) copy-start(bf16[512,128]{1,0:T(8,128)(2,1)} %get-tuple-element.1147) | copy-start | bytes 393220 | tf_op jit(solution)/shard_map/while
  352.4 18.7 %copy-start.7 = (bf16[512,128]{1,0:T(8,128)(2,1)S(1)}, bf16[512,128]{1,0:T(8,128)(2,1)}, u32[]{:S(2)}) copy-start(bf16[512,128]{1,0:T(8,128)(2,1)} %param.16) | copy-start | bytes 393220
  352.5 71.4 %all-gather.11.cloned.1.call-start = ((), (), s32[]{:S(2)}) async-start(), calls=%async_computation.1 | async-start | bytes 1179648 | tf_op jit(solution)/shard_map/all_gather | solution.py:163
  353.2 95.7 %all-gather.13.cloned.1.call-start = ((), (), s32[]{:S(2)}) async-start(), calls=%async_computation.2 | async-start | bytes 1179648 | tf_op jit(solution)/shard_map/all_gather | solution.py:164
  353.9 672.5 %all-reduce.5.cloned.1.call-start = ((), (), s32[]{:S(2)}) async-start(), calls=%async_computation.5 | async-start | bytes 262144
  472.0 2.5 copy-start
  472.0 4.2 copy-start.5
  474.5 3.2 copy-start.2
  476.1 3.1 copy-start.1
  479.3 13.0 %copy-start.3 = (f32[1024,128]{1,0:T(8,128)}, f32[1024,128]{1,0:T(8,128)S(1)}, u32[]{:S(2)}) copy-start(f32[1024,128]{1,0:T(8,128)S(1)} %convolution_add_fusion.4) | copy-start | bytes 1572868 | tf_op jit(solution)/shard_map/while
  502.4 3.6 copy-start.9
  506.1 2.0 copy-start.8
  528.4 2.5 copy-start
  528.4 4.2 copy-start.5
  531.0 3.2 copy-start.2
  532.6 3.1 copy-start.1
  535.7 13.0 %copy-start.3 = (f32[1024,128]{1,0:T(8,128)}, f32[1024,128]{1,0:T(8,128)S(1)}, u32[]{:S(2)}) copy-start(f32[1024,128]{1,0:T(8,128)S(1)} %convolution_add_fusion.4) | copy-start | bytes 1572868 | tf_op jit(solution)/shard_map/while
  558.9 3.6 copy-start.9
  562.5 2.0 copy-start.8
  584.9 2.5 copy-start
  584.9 4.2 copy-start.5
  587.4 3.2 copy-start.2
  589.1 3.1 copy-start.1
  592.2 13.0 %copy-start.3 = (f32[1024,128]{1,0:T(8,128)}, f32[1024,128]{1,0:T(8,128)S(1)}, u32[]{:S(2)}) copy-start(f32[1024,128]{1,0:T(8,128)S(1)} %convolution_add_fusion.4) | copy-start | bytes 1572868 | tf_op jit(solution)/shard_map/while
  615.4 3.6 copy-start.9
  619.0 2.0 copy-start.8
  641.4 2.5 copy-start
  641.4 4.2 copy-start.5
  643.9 3.2 copy-start.2
  645.6 3.1 copy-start.1
  648.7 13.0 %copy-start.3 = (f32[1024,128]{1,0:T(8,128)}, f32[1024,128]{1,0:T(8,128)S(1)}, u32[]{:S(2)}) copy-start(f32[1024,128]{1,0:T(8,128)S(1)} %convolution_add_fusion.4) | copy-start | bytes 1572868 | tf_op jit(solution)/shard_map/while
  671.9 3.6 copy-start.9
  675.5 2.0 copy-start.8
  697.9 2.5 copy-start
  697.9 4.2 copy-start.5
  700.4 3.2 copy-start.2
  702.0 3.1 copy-start.1
  705.1 13.0 %copy-start.3 = (f32[1024,128]{1,0:T(8,128)}, f32[1024,128]{1,0:T(8,128)S(1)}, u32[]{:S(2)}) copy-start(f32[1024,128]{1,0:T(8,128)S(1)} %convolution_add_fusion.4) | copy-start | bytes 1572868 | tf_op jit(solution)/shard_map/while
  728.3 3.6 copy-start.9
  732.0 2.0 copy-start.8
  754.3 2.5 copy-start
  754.3 4.2 copy-start.5
  756.9 3.2 copy-start.2
  758.5 3.1 copy-start.1
  761.6 13.0 %copy-start.3 = (f32[1024,128]{1,0:T(8,128)}, f32[1024,128]{1,0:T(8,128)S(1)}, u32[]{:S(2)}) copy-start(f32[1024,128]{1,0:T(8,128)S(1)} %convolution_add_fusion.4) | copy-start | bytes 1572868 | tf_op jit(solution)/shard_map/while
  784.8 3.6 copy-start.9
  810.8 2.5 copy-start
  810.8 4.2 copy-start.5
  813.3 3.2 copy-start.2
  815.0 3.1 copy-start.1
  818.1 13.0 %copy-start.3 = (f32[1024,128]{1,0:T(8,128)}, f32[1024,128]{1,0:T(8,128)S(1)}, u32[]{:S(2)}) copy-start(f32[1024,128]{1,0:T(8,128)S(1)} %convolution_add_fusion.4) | copy-start | bytes 1572868 | tf_op jit(solution)/shard_map/while
  841.3 3.6 copy-start.9
  867.3 2.5 copy-start
  867.3 4.2 copy-start.5
  869.8 3.2 copy-start.2
  871.4 3.1 copy-start.1
  874.6 13.0 %copy-start.3 = (f32[1024,128]{1,0:T(8,128)}, f32[1024,128]{1,0:T(8,128)S(1)}, u32[]{:S(2)}) copy-start(f32[1024,128]{1,0:T(8,128)S(1)} %convolution_add_fusion.4) | copy-start | bytes 1572868 | tf_op jit(solution)/shard_map/while
  897.8 3.6 copy-start.9
  901.4 4.0 copy-start.4
  903.1 262.5 %reduce-scatter.2.cloned.1.call-start = ((), (), s32[]{:S(2)}) async-start(), calls=%async_computation.3 | async-start | bytes 2162688 | tf_op jit(solution)/shard_map/reduce_scatter | solution.py:218
  (20 other events, 34.7 us)
Sparse Core Ops, SparseCore 0:
  352.6 12.8 all-gather.14
  367.6 40.4 all-gather.10
  410.2 38.6 all-gather.12
  903.2 123.1 all-reduce.4
  1028.5 136.9 reduce-scatter.1
where the time goes:
time: 1190 us; the launch traced here: 1170 us
  local copies, waits for them, and re-layouts  622 us (52%)
  waiting for transfers between devices  285 us (24%)
  blocking collectives  107 us (9%)
  matrix products  89.8 us (8%)
  other arithmetic  41.6 us (3%)
  between operations  14.5 us (1%)
  loops' own time  13.8 us (1%)
    rev x12, local copies, waits for them, and re-layouts, toeplitz_rows(): return tiled[::-1, :col_count]  222 us
    reduce_scatter x1, waiting for transfers between devices, on_device(): lax.psum_scatter(query_pieces.reshape(total_rows, head_dim), ('pb', 'ka')...  138 us
    unnamed x6, waiting for transfers between devices  122 us
    rev x8, local copies, waits for them, and re-layouts, diagonal_sums(): flipped = dscore_mat[:, ::-1]  94.6 us
    another operation x24, local copies, waits for them, and re-layouts, toeplitz_rows(): jnp.tile(backward, row_count + 1)[:row_count * (length + 1)]  78.7 us
    reshape x16, local copies, waits for them, and re-layouts, diagonal_sums(): skewed = padded.reshape(-1)[:row_count * length].reshape(row_count, length)  52 us
    all_gather x1, blocking collectives, on_device(): bias_whole = lax.all_gather(bias, ('pb', 'ka'), axis=0, tiled=True)  43.9 us
    reshape x12, local copies, waits for them, and re-layouts, toeplitz_rows(): jnp.tile(backward, row_count + 1)[:row_count * (length + 1)]  42.4 us
  transfers between devices with their start and end apart: 5, of which 3 were waited for; matrix products, arithmetic and copies ran while one was open for 1% of the time, Pallas kernels for 0%

commit v1 on v0

v1 whole, which is shorter than its diff:
```python
import math

import jax
import jax.numpy as jnp
from jax import lax
from jax.experimental import pallas as pl
from jax.experimental.pallas import tpu as pltpu
from jax.sharding import PartitionSpec as P

LANES = 128
NEGATIVE = -1e30
FLOOR = -1e20
LOG2E = math.log2(math.e)
MESH = pl.DeviceIdType.MESH
VMEM = pl.BlockSpec(memory_space=pltpu.VMEM)


def dot_nt(a, b):
    return lax.dot_general(a, b, (((1,), (1,)), ((), ())), preferred_element_type=jnp.float32)


def dot_nn(a, b):
    return jnp.dot(a, b, preferred_element_type=jnp.float32)


def me_and_count(pb_size, ka_size):
    return lax.axis_index("pb") * ka_size + lax.axis_index("ka"), pb_size * ka_size


def peer_id(linear, ka_size):
    return (linear // ka_size, lax.rem(linear, ka_size))


def greet_all(me, count, ka_size):
    barrier = pltpu.get_barrier_semaphore()
    for k in range(1, count):
        pl.semaphore_signal(
            barrier, inc=1, device_id=peer_id(lax.rem(me + k, count), ka_size), device_id_type=MESH
        )
    pl.semaphore_wait(barrier, count - 1)


def push_all(src_of, dst_ref, send_sems, recv_sems, me, count, ka_size):
    copies = []
    for k in range(1, count):
        peer = lax.rem(me + k, count)
        copy = pltpu.make_async_remote_copy(
            src_ref=src_of(peer),
            dst_ref=dst_ref.at[me],
            send_sem=send_sems.at[k],
            recv_sem=recv_sems.at[k],
            device_id=peer_id(peer, ka_size),
            device_id_type=MESH,
        )
        copy.start()
        copies.append(copy)
    return copies


def gather_kernel(pb_size, ka_size, x_ref, out_ref, send_sems, recv_sems):
    me, count = me_and_count(pb_size, ka_size)
    greet_all(me, count, ka_size)
    copies = push_all(lambda peer: x_ref, out_ref, send_sems, recv_sems, me, count, ka_size)
    out_ref[me] = x_ref[...]
    for copy in copies:
        copy.wait()


def gather_small(x, pb_size, ka_size, collective_id):
    count = pb_size * ka_size
    return pl.pallas_call(
        lambda *refs: gather_kernel(pb_size, ka_size, *refs),
        out_shape=jax.ShapeDtypeStruct((count,) + x.shape, x.dtype),
        in_specs=[VMEM],
        out_specs=VMEM,
        scratch_shapes=[pltpu.SemaphoreType.DMA((count,)), pltpu.SemaphoreType.DMA((count,))],
        compiler_params=pltpu.CompilerParams(collective_id=collective_id, has_side_effects=True),
        name=f"gather_{collective_id}",
    )(x)


def entry_kernel(
    pb_size, ka_size, bias_ref, rows_ref, bias_out, rows_out,
    bias_send, bias_recv, pb_send, pb_recv, y_send, y_recv, core_sems,
):
    me, count = me_and_count(pb_size, ka_size)
    pb, ka = lax.axis_index("pb"), lax.axis_index("ka")
    y_size = ka_size // 2
    y, core = ka // 2, lax.rem(ka, 2)
    greet_all(me, count, ka_size)
    stage_one = []
    for k in range(1, pb_size):
        copy = pltpu.make_async_remote_copy(
            src_ref=rows_ref,
            dst_ref=rows_out.at[core, y, pb],
            send_sem=pb_send.at[k],
            recv_sem=pb_recv.at[k],
            device_id=(lax.rem(pb + k, pb_size), ka),
            device_id_type=MESH,
        )
        copy.start()
        stage_one.append(copy)
    bias_copies = push_all(lambda peer: bias_ref, bias_out, bias_send, bias_recv, me, count, ka_size)
    rows_out[core, y, pb] = rows_ref[...]
    bias_out[me] = bias_ref[...]
    for copy in stage_one:
        copy.wait()
    stage_two = []
    for k in range(1, y_size):
        copy = pltpu.make_async_remote_copy(
            src_ref=rows_out.at[core, y],
            dst_ref=rows_out.at[core, y],
            send_sem=y_send.at[k],
            recv_sem=y_recv.at[k],
            device_id=(pb, lax.rem(y + k, y_size) * 2 + core),
            device_id_type=MESH,
        )
        copy.start()
        stage_two.append(copy)
    for copy in bias_copies:
        copy.wait()
    for copy in stage_two:
        copy.wait()
    copy = pltpu.make_async_remote_copy(
        src_ref=rows_out.at[core],
        dst_ref=rows_out.at[core],
        send_sem=core_sems.at[0],
        recv_sem=core_sems.at[1],
        device_id=(pb, y * 2 + 1 - core),
        device_id_type=MESH,
    )
    copy.start()
    copy.wait()


def entry_gather(bias, rows, pb_size, ka_size):
    count = pb_size * ka_size
    dma = pltpu.SemaphoreType.DMA
    return pl.pallas_call(
        lambda *refs: entry_kernel(pb_size, ka_size, *refs),
        out_shape=(
            jax.ShapeDtypeStruct((count,) + bias.shape, bias.dtype),
            jax.ShapeDtypeStruct((2, ka_size // 2, pb_size) + rows.shape, rows.dtype),
        ),
        in_specs=[VMEM, VMEM],
        out_specs=(VMEM, VMEM),
        scratch_shapes=[
            dma((count,)), dma((count,)), dma((pb_size,)), dma((pb_size,)),
            dma((ka_size,)), dma((ka_size,)), dma((2,)),
        ],
        compiler_params=pltpu.CompilerParams(collective_id=0, has_side_effects=True),
        name="entry_gather",
    )(bias, rows)


def exit_kernel(
    pb_size, ka_size, scale, dq_ref, bias_ref, dq_out, bias_out,
    dq_slots, bias_slots, dq_send, dq_recv, bias_send, bias_recv,
):
    me, count = me_and_count(pb_size, ka_size)
    greet_all(me, count, ka_size)
    copies = push_all(lambda peer: dq_ref.at[peer], dq_slots, dq_send, dq_recv, me, count, ka_size)
    copies += push_all(
        lambda peer: bias_ref.at[peer], bias_slots, bias_send, bias_recv, me, count, ka_size
    )
    dq_slots[me] = dq_ref[me]
    bias_slots[me] = bias_ref[me]
    for copy in copies:
        copy.wait()
    total = dq_slots[0].astype(jnp.float32)
    diag = bias_slots[0]
    for k in range(1, count):
        total = total + dq_slots[k].astype(jnp.float32)
        diag = diag + bias_slots[k]
    dq_out[...] = (total.T * scale).astype(dq_out.dtype)
    bias_out[...] = diag


def exit_reduce(dq, bias, scale, pb_size, ka_size):
    count = pb_size * ka_size
    dma = pltpu.SemaphoreType.DMA
    return pl.pallas_call(
        lambda *refs: exit_kernel(pb_size, ka_size, scale, *refs),
        out_shape=(
            jax.ShapeDtypeStruct((dq.shape[2], dq.shape[1]), jnp.bfloat16),
            jax.ShapeDtypeStruct(bias.shape[1:], jnp.float32),
        ),
        in_specs=[VMEM, VMEM],
        out_specs=(VMEM, VMEM),
        scratch_shapes=[
            pltpu.VMEM(dq.shape, dq.dtype), pltpu.VMEM(bias.shape, bias.dtype),
            dma((count,)), dma((count,)), dma((count,)), dma((count,)),
        ],
        compiler_params=pltpu.CompilerParams(collective_id=2, has_side_effects=True),
        name="exit_reduce",
    )(dq, bias)


def build_table(w_ref, t_ref, tiles):
    def one(t, carry):
        first = w_ref[pl.ds(tiles - 1 - t, 1), :]
        second = w_ref[pl.ds(tiles - t, 1), :]
        wide = jnp.broadcast_to(jnp.concatenate([first, second], axis=1), (LANES, 2 * LANES))
        turned = pltpu.roll(wide, LANES + 1, axis=1, stride=1, stride_axis=0)
        t_ref[pl.ds(pl.multiple_of(t * LANES, LANES), LANES), :] = turned[:, :LANES]
        return carry

    lax.fori_loop(0, tiles, one, 0)


def forward_kernel(
    key_rows, factor, w_ref, q_ref, g_ref, k_ref, v_ref, out_ref, t_ref, m_ref, l_ref, d_ref
):
    step = pl.program_id(0)
    chunk = k_ref.shape[0]
    blocks = q_ref.shape[0] // LANES
    tiles = t_ref.shape[0] // LANES

    @pl.when(step == 0)
    def _():
        build_table(w_ref, t_ref, tiles)
        m_ref[...] = jnp.full_like(m_ref, FLOOR)
        l_ref[...] = jnp.zeros_like(l_ref)
        d_ref[...] = jnp.zeros_like(d_ref)

    def one(kb, carry):
        at = pl.multiple_of(kb * key_rows, key_rows)
        scores = dot_nt(k_ref[pl.ds(at, key_rows), :], q_ref[...])
        dprobs = dot_nt(v_ref[pl.ds(at, key_rows), :], g_ref[...])
        for b in range(blocks):
            lanes = slice(b * LANES, (b + 1) * LANES)
            kappa = pl.multiple_of(step * chunk + at + LANES * (blocks - 1 - b), LANES)
            s = scores[:, lanes] * factor + t_ref[pl.ds(kappa, key_rows), :]
            s = s.reshape(key_rows // 8, 8, LANES)
            d = dprobs[:, lanes].reshape(key_rows // 8, 8, LANES)
            old = m_ref[:, lanes]
            new = jnp.maximum(old, jnp.max(s, axis=0))
            e = jnp.exp2(s - new[None])
            alpha = jnp.exp2(old - new)
            m_ref[:, lanes] = new
            l_ref[:, lanes] = l_ref[:, lanes] * alpha + jnp.sum(e, axis=0)
            d_ref[:, lanes] = d_ref[:, lanes] * alpha + jnp.sum(e * d, axis=0)
        return carry

    lax.fori_loop(0, chunk // key_rows, one, 0)

    @pl.when(step == pl.num_programs(0) - 1)
    def _():
        m = m_ref[...]
        top = jnp.max(m, axis=0, keepdims=True)
        share = jnp.exp2(m - top)
        out_ref[0:1, :] = top
        out_ref[1:2, :] = jnp.sum(l_ref[...] * share, axis=0, keepdims=True)
        out_ref[2:3, :] = jnp.sum(d_ref[...] * share, axis=0, keepdims=True)
        out_ref[3:4, :] = jnp.zeros_like(top)


def forward(window, queries, grads, keys, values, factor):
    rows, dim = queries.shape
    count = keys.shape[0]
    chunk = min(1024, count)
    tiles = count // LANES + rows // LANES - 1
    whole = lambda i: (0, 0)
    return pl.pallas_call(
        lambda *refs: forward_kernel(min(256, chunk), factor, *refs),
        out_shape=jax.ShapeDtypeStruct((4, rows), jnp.float32),
        grid=(count // chunk,),
        in_specs=[
            pl.BlockSpec(window.shape, whole),
            pl.BlockSpec((rows, dim), whole),
            pl.BlockSpec((rows, dim), whole),
            pl.BlockSpec((chunk, dim), lambda i: (i, 0)),
            pl.BlockSpec((chunk, dim), lambda i: (i, 0)),
        ],
        out_specs=pl.BlockSpec((4, rows), whole),
        scratch_shapes=[
            pltpu.VMEM((tiles * LANES, LANES), jnp.float32),
            pltpu.VMEM((8, rows), jnp.float32),
            pltpu.VMEM((8, rows), jnp.float32),
            pltpu.VMEM((8, rows), jnp.float32),
        ],
        name="forward",
    )(window, queries, grads, keys, values)


def fold_diagonals(g_ref, diag_ref, tiles):
    diag_ref[...] = jnp.zeros_like(diag_ref)

    def one(t, carry):
        tile = g_ref[pl.ds(pl.multiple_of(t * LANES, LANES), LANES), :]
        x = jnp.concatenate([tile, jnp.zeros_like(tile)], axis=1)
        half = LANES // 2
        while half >= 8:
            x = pltpu.roll(x[:half], half, axis=1) + x[half:]
            half //= 2
        for part in (4, 2, 1):
            x = pltpu.roll(x, part, axis=1) + pltpu.roll(x, 8 - part, axis=0)
        low = pl.ds(tiles - 1 - t, 1)
        high = pl.ds(tiles - t, 1)
        diag_ref[low, :] = diag_ref[low, :] + x[0:1, :LANES]
        diag_ref[high, :] = diag_ref[high, :] + x[0:1, LANES:]
        return carry

    lax.fori_loop(0, tiles, one, 0)


def backward_kernel(
    key_rows, factor, scale, w_ref, rows_ref, lse_ref, dots_ref, k_ref, v_ref, kt_ref,
    dq_ref, dk_ref, dv_ref, diag_ref, t_ref, g_ref, dk_acc, dv_acc, dq_acc,
):
    step = pl.program_id(0)
    dim = k_ref.shape[1]
    chunk = lse_ref.shape[1]
    blocks = chunk // LANES
    tiles = t_ref.shape[0] // LANES
    last_block = tiles - k_ref.shape[0] // LANES

    @pl.when(step == 0)
    def _():
        build_table(w_ref, t_ref, tiles)
        g_ref[...] = jnp.zeros_like(g_ref)
        dk_acc[...] = jnp.zeros_like(dk_acc)
        dv_acc[...] = jnp.zeros_like(dv_acc)

    rows = rows_ref[...].reshape(chunk, 2 * dim)
    q, g = rows[:, :dim], rows[:, dim:]
    dq_acc[...] = jnp.zeros_like(dq_acc)

    def one(kb, carry):
        at = pl.multiple_of(kb * key_rows, key_rows)
        here = pl.ds(at, key_rows)
        scores = dot_nt(k_ref[here, :], q)
        dprobs = dot_nt(v_ref[here, :], g)
        probs_low, dscores_low = [], []
        for b in range(blocks):
            lanes = slice(b * LANES, (b + 1) * LANES)
            kappa = pl.multiple_of(at + LANES * (last_block - step * blocks - b), LANES)
            there = pl.ds(kappa, key_rows)
            s = scores[:, lanes] * factor + t_ref[there, :]
            p = jnp.exp2(s - lse_ref[:, lanes])
            ds = p * (dprobs[:, lanes] - dots_ref[:, lanes])
            g_ref[there, :] = g_ref[there, :] + ds
            probs_low.append(p.astype(jnp.bfloat16))
            dscores_low.append(ds.astype(jnp.bfloat16))
        p_low = jnp.concatenate(probs_low, axis=1)
        ds_low = jnp.concatenate(dscores_low, axis=1)
        dv_acc[here, :] += dot_nn(p_low, g)
        dk_acc[here, :] += dot_nn(ds_low, q)
        dq_acc[...] += dot_nn(kt_ref[kb], ds_low)
        return carry

    lax.fori_loop(0, k_ref.shape[0] // key_rows, one, 0)

    width = dq_ref.shape[2]
    for b in range(chunk // width):
        dq_ref[b] = dq_acc[:, b * width : (b + 1) * width].astype(dq_ref.dtype)

    @pl.when(step == pl.num_programs(0) - 1)
    def _():
        dk_ref[...] = (dk_acc[...] * scale).astype(dk_ref.dtype)
        dv_ref[...] = dv_acc[...].astype(dv_ref.dtype)
        fold_diagonals(g_ref, diag_ref, tiles)


def backward(window, rows, lse, dots, keys, values, factor, scale):
    parts, steps, part_rows, wide = rows.shape
    count, dim = keys.shape
    chunk = parts * part_rows
    tiles = count // LANES + steps * chunk // LANES - 1
    key_rows = min(256, count)
    keys_turned = keys.reshape(count // key_rows, key_rows, dim).swapaxes(1, 2)
    whole = lambda i: (0, 0)
    f32 = jnp.float32
    return pl.pallas_call(
        lambda *refs: backward_kernel(key_rows, factor, scale, *refs),
        out_shape=(
            jax.ShapeDtypeStruct((parts * steps, dim, part_rows), jnp.bfloat16),
            jax.ShapeDtypeStruct((count, dim), jnp.bfloat16),
            jax.ShapeDtypeStruct((count, dim), jnp.bfloat16),
            jax.ShapeDtypeStruct(window.shape, f32),
        ),
        grid=(steps,),
        in_specs=[
            pl.BlockSpec(window.shape, whole),
            pl.BlockSpec((parts, 1, part_rows, wide), lambda i: (0, i, 0, 0)),
            pl.BlockSpec((1, chunk), lambda i: (0, i)),
            pl.BlockSpec((1, chunk), lambda i: (0, i)),
            pl.BlockSpec((count, dim), whole),
            pl.BlockSpec((count, dim), whole),
            pl.BlockSpec(keys_turned.shape, lambda i: (0, 0, 0)),
        ],
        out_specs=(
            pl.BlockSpec((parts, dim, part_rows), lambda i: (i, 0, 0)),
            pl.BlockSpec((count, dim), whole),
            pl.BlockSpec((count, dim), whole),
            pl.BlockSpec(window.shape, whole),
        ),
        scratch_shapes=[
            pltpu.VMEM((tiles * LANES, LANES), f32),
            pltpu.VMEM((tiles * LANES, LANES), f32),
            pltpu.VMEM((count, dim), f32),
            pltpu.VMEM((count, dim), f32),
            pltpu.VMEM((dim, chunk), f32),
        ],
        name="backward",
    )(window, rows, lse, dots, keys, values, keys_turned)


def on_device(queries, keys, values, bias, grad_out, group_start):
    pb_size, ka_size = lax.axis_size("pb"), lax.axis_size("ka")
    pb, ka = lax.axis_index("pb"), lax.axis_index("ka")
    rows, dim = queries.shape
    key_count = keys.shape[0]
    total_rows = rows * pb_size
    scale = dim ** (-0.5)
    factor = scale * LOG2E
    first = group_start[0]

    part_rows = rows // ka_size
    both = jnp.concatenate([queries, grad_out], axis=1)
    own_rows = lax.dynamic_slice_in_dim(both, ka * part_rows, part_rows, 0)
    bias_all, row_all = entry_gather(bias.reshape(-1, LANES), own_rows, pb_size, ka_size)
    row_all = row_all.swapaxes(0, 1).reshape(ka_size, pb_size, part_rows, 2 * dim)

    bias_count = bias.shape[0] * pb_size * ka_size
    margin = key_count * ka_size
    tail = 2 * LANES
    table = jnp.concatenate(
        [
            jnp.full((margin,), NEGATIVE, jnp.float32),
            bias_all.reshape(-1) * LOG2E,
            jnp.zeros((tail,), jnp.float32),
        ]
    )

    def window_of(query_first, key_first, query_rows, key_rows):
        low = query_first - key_first - key_rows + 1 + margin
        size = key_rows + query_rows
        return low, lax.dynamic_slice_in_dim(table, low, size).reshape(-1, LANES)

    key_base = ka * key_count
    low, window = window_of(first + pb * rows, key_base, rows, key_count)
    stats = forward(window, queries, grad_out, keys, values, factor)
    stats_all = gather_small(stats.reshape(-1, LANES), pb_size, ka_size, 1)
    stats_all = stats_all.reshape(pb_size, ka_size, 4, rows)
    top = jnp.max(stats_all[:, :, 0], axis=1)
    share = jnp.exp2(stats_all[:, :, 0] - top[:, None])
    row_sum = jnp.sum(stats_all[:, :, 1] * share, axis=1)
    lse = (top + jnp.log2(row_sum)).reshape(1, total_rows)
    dots = (jnp.sum(stats_all[:, :, 2] * share, axis=1) / row_sum).reshape(1, total_rows)

    own_count = key_count // pb_size
    own_keys = lax.dynamic_slice_in_dim(keys, pb * own_count, own_count, 0)
    own_values = lax.dynamic_slice_in_dim(values, pb * own_count, own_count, 0)
    low, window = window_of(first, key_base + pb * own_count, total_rows, own_count)
    dq, key_grad, value_grad, diag = backward(
        window, row_all, lse, dots, own_keys, own_values, factor, scale
    )
    spread = lax.dynamic_update_slice_in_dim(
        jnp.zeros(table.shape, jnp.float32), diag.reshape(-1), low, 0
    )
    spread = spread[margin : margin + bias_count].reshape(pb_size * ka_size, -1, LANES)
    query_grad, bias_grad = exit_reduce(dq, spread, scale, pb_size, ka_size)
    return query_grad, key_grad, value_grad, bias_grad.reshape(-1)


def solution(mesh):
    return jax.shard_map(
        on_device,
        mesh=mesh,
        in_specs=(P("pb", None), P("ka", None), P("ka", None), P(("pb", "ka")), P("pb", None), P()),
        out_specs=(
            P(("pb", "ka"), None),
            P(("ka", "pb"), None),
            P(("ka", "pb"), None),
            P(("pb", "ka")),
        ),
        check_vma=False,
    )
```

time: 1190 us -> 167 us (0.14); the launches traced: 1170 us -> 167 us
  local copies, waits for them, and re-layouts: 622 us -> 15 us
  waiting for transfers between devices: 285 us -> 0 us
  Pallas kernels: 0 us -> 147 us
  blocking collectives: 107 us -> 0 us
  matrix products: 89.8 us -> 0 us
  other arithmetic: 41.6 us -> 2.67 us
  loops' own time: 13.8 us -> 0 us
  between operations: 14.5 us -> 1.4 us
    rev x20 -> x0, local copies, waits for them, and re-layouts: 316 us -> none  [the longest x12 222 us: toeplitz_rows(): return tiled[::-1, :col_count]]
    pallas_call x0 -> x5, Pallas kernels: none -> 147 us  [the longest x1 42.5 us: backward(): pl.pallas_call(lambda *refs: backward_kernel(key_rows, factor, scale, *re...]
    reduce_scatter x1 -> x0, waiting for transfers between devices: 138 us -> none  [on_device(): lax.psum_scatter(query_pieces.reshape(total_rows, head_dim), ('pb', 'ka')...]
    unnamed x6 -> x0, waiting for transfers between devices: 122 us -> none
    all_gather x5 -> x0, blocking collectives: 107 us -> none  [the longest x1 43.9 us: on_device(): bias_whole = lax.all_gather(bias, ('pb', 'ka'), axis=0, tiled=True)]
    dot_general x48 -> x0, matrix products: 89.8 us -> none  [the longest x12 33.8 us: block_scores(): jnp.einsum('qd,kd->qk', query_block, key_block, preferred_element_type=jn...]
    reshape x28 -> x6, local copies, waits for them, and re-layouts: 94.4 us -> 5.21 us  [the longest x2 1.38 us: window_of(): return (low, lax.dynamic_slice_in_dim(table, low, size).reshape(-1, LANES))]
    another operation x24 -> x0, local copies, waits for them, and re-layouts: 78.7 us -> none  [toeplitz_rows(): jnp.tile(backward, row_count + 1)[:row_count * (length + 1)]]
  transfers between devices with their start and end apart: 5 -> 0, of which waited for: 3 -> 0; matrix products, arithmetic and copies ran while one was open for 1% -> 0% of each run, Pallas kernels for 0% -> 0%
where the time goes in v1:
time: 167 us
  Pallas kernels  147 us (88%)
  local copies, waits for them, and re-layouts  15 us (9%)
  other arithmetic  2.67 us (2%)
    pallas_call x1, Pallas kernels, backward(): pl.pallas_call(lambda *refs: backward_kernel(key_rows, factor, scale, *re...  42.5 us
    pallas_call x1, Pallas kernels, exit_reduce(): pl.pallas_call(lambda *refs: exit_kernel(pb_size, ka_size, scale, *refs),...  36 us
    pallas_call x1, Pallas kernels, entry_gather(): pl.pallas_call(lambda *refs: entry_kernel(pb_size, ka_size, *refs), out_s...  34.2 us
    pallas_call x1, Pallas kernels, forward(): pl.pallas_call(lambda *refs: forward_kernel(min(256, chunk), factor, *ref...  19.3 us
    pallas_call x1, Pallas kernels, gather_small(): pl.pallas_call(lambda *refs: gather_kernel(pb_size, ka_size, *refs), out_...  15.5 us
    unnamed x6, local copies, waits for them, and re-layouts  3.87 us

profile of v1, /device:TPU:0, one launch (start us, length us, event | category | flops | bytes accessed | tf_op | source)
XLA Modules:
  0.0 166.5 jit_solution(16957876093064422058)
XLA Ops:
  0.6 1.4 fusion.refs_1_
  2.1 34.2 %entry_gather.1 = (f32[32,8,128]{2,1,0:T(8,128)}, bf16[2,2,8,128,256]{4,3,2,1,0:T(8,128)(2,1)}) custom-call(f32[8,128]{1,0:T(8,128)} %bitcast.55, bf16[128,256]{1,0:T(8,128)(2,1)} %fusion.refs_1_), custom_call_target="tpu_custom_call" | custom-call | tf_op jit(solution)/shard_map/entry_gather/pallas_call | solution.py:139
  36.2 0.9 multiply_bitcast_fusion
  37.9 0.7 dynamic-slice_bitcast_fusion.1.refs_0_
  38.6 3.2 %copy.13 = bf16[2,2,8,128,256]{4,3,2,1,0:T(8,128)(2,1)} copy(bf16[2,2,8,128,256]{4,3,2,0,1:T(8,128)(2,1)} %bitcast.51) | data formatting | bytes 4194304 | tf_op jit(solution)/shard_map/transpose | solution.py:423
  41.7 0.7 dynamic-slice_bitcast_fusion.refs_0_
  42.4 19.3 %forward.1 = f32[4,512]{1,0:T(4,128)} custom-call(f32[68,128]{1,0:T(8,128)} %dynamic-slice_bitcast_fusion.refs_0_, bf16[512,128]{1,0:T(8,128)(2,1)} %refs_1_.1, bf16[512,128]{1,0:T(8,128)(2,1)} %refs_2_.1, bf16[8192,128]{1,0:T(8,128)(2,1)} %refs_3_.1, bf16[8192,128]{1,0:T(8,128)(2,1)} %refs_4_.1), custom_call_target="tpu_custom_call" | custom-call | tf_op jit(solution)/shard_map/forward/pallas_call | solution.py:264
  61.8 1.3 reshape.93.refs_0_
  63.1 15.5 %gather_1.1 = f32[32,16,128]{2,1,0:T(8,128)} custom-call(f32[16,128]{1,0:T(8,128)} %reshape.93.refs_0_), custom_call_target="tpu_custom_call" | custom-call | tf_op jit(solution)/shard_map/gather_1/pallas_call | solution.py:71
  78.6 1.0 reshape.94
  79.6 0.2 fusion.7
  79.8 0.1 fusion.6
  79.9 0.6 copy.21
  80.6 0.6 copy.22
  81.2 1.8 %constant_dynamic-slice_fusion = (bf16[1024,128]{1,0:T(8,128)(2,1)}, bf16[1024,128]{1,0:T(8,128)(2,1)S(1)}) fusion(bf16[8192,128]{1,0:T(8,128)(2,1)} %refs_4_.1, s32[]{:T(128)S(6)} %select_n.17, bf16[8192,128]{1,0:T(8,128)(2,1)} %refs_3_.1), kind=kLoop, calls=%fused_computation.20 | loop fusion | bytes 1048580 | tf_op jit(solution)/shard_map/dynamic_slice | solution.py:454
  83.0 0.0 copy-start
  83.0 0.8 copy.16
  83.8 0.0 copy-done
  83.8 42.5 %backward.1 = (bf16[32,128,128]{2,1,0:T(8,128)(2,1)}, bf16[1024,128]{1,0:T(8,128)(2,1)}, bf16[1024,128]{1,0:T(8,128)(2,1)}, f32[40,128]{1,0:T(8,128)}) custom-call(f32[40,128]{1,0:T(8,128)} %dynamic-slice_bitcast_fusion.1.refs_0_, bf16[4,8,128,256]{3,2,1,0:T(8,128)(2,1)} %bitcast.49, f32[1,4096]{1,0:T(1,128)} %bitcast.53, f32[1,4096]{1,0:T(1,128)} %bitcast.54, ...), custom_call_target="tpu_custom_call" | custom-call | tf_op jit(solution)/shard_map/backward/pallas_call | solution.py:374
  126.3 0.9 bitcast_dynamic-update-slice_fusion
  127.2 0.6 slice_bitcast_fusion.refs_1_
  127.9 36.0 %exit_reduce.1 = (bf16[128,128]{1,0:T(8,128)(2,1)}, f32[8,128]{1,0:T(8,128)}) custom-call(bf16[32,128,128]{2,1,0:T(8,128)(2,1)} %get-tuple-element.14.refs_0_, f32[32,8,128]{2,1,0:T(8,128)} %slice_bitcast_fusion.refs_1_), custom_call_target="tpu_custom_call" | custom-call | tf_op jit(solution)/shard_map/exit_reduce/pallas_call | solution.py:182
  163.9 1.4 copy.44
  165.2 1.3 copy.45
  (5 shorter events, 0.1 us)
Async XLA Ops:
  83.0 0.8 copy-start

commit v2 on v1

v2 whole, which is shorter than its diff:
```python
import math

import jax
import jax.numpy as jnp
from jax import lax
from jax.experimental import pallas as pl
from jax.experimental.pallas import tpu as pltpu
from jax.sharding import PartitionSpec as P

LANES = 128
NEGATIVE = -1e30
FLOOR = -1e20
LOG2E = math.log2(math.e)
MESH = pl.DeviceIdType.MESH
VMEM = pl.BlockSpec(memory_space=pltpu.VMEM)


def dot_nt(a, b):
    return lax.dot_general(a, b, (((1,), (1,)), ((), ())), preferred_element_type=jnp.float32)


def dot_nn(a, b):
    return jnp.dot(a, b, preferred_element_type=jnp.float32)


def signal_peers(peers):
    barrier = pltpu.get_barrier_semaphore()
    for peer in peers:
        pl.semaphore_signal(barrier, inc=1, device_id=peer, device_id_type=MESH)


def await_peers(count):
    pl.semaphore_wait(pltpu.get_barrier_semaphore(), count)


def push(src, dst, send_sem, recv_sem, peer):
    return pltpu.make_async_remote_copy(
        src_ref=src, dst_ref=dst, send_sem=send_sem, recv_sem=recv_sem,
        device_id=peer, device_id_type=MESH,
    )


def pb_peers(pb, ka, pb_size):
    return [(lax.rem(pb + k, pb_size), ka) for k in range(1, pb_size)]


def ka_peers(pb, ka, ka_size):
    return [(pb, lax.rem(ka + k, ka_size)) for k in range(1, ka_size)]


def run_all(copies):
    for copy in copies:
        copy.start()
    return copies


def wait_all(copies):
    for copy in copies:
        copy.wait()


dma = pltpu.SemaphoreType.DMA


def small_call(body, out_shape, scratch, collective_id, name, *operands):
    return pl.pallas_call(
        body,
        out_shape=out_shape,
        in_specs=[VMEM] * len(operands),
        out_specs=VMEM,
        scratch_shapes=scratch,
        compiler_params=pltpu.CompilerParams(collective_id=collective_id, has_side_effects=True),
        name=name,
    )(*operands)


def bias_gather(bias, pb_size, ka_size):
    def body(x_ref, out_ref, pb_send, pb_recv, ka_send, ka_recv):
        pb, ka = lax.axis_index("pb"), lax.axis_index("ka")
        over_pb, over_ka = pb_peers(pb, ka, pb_size), ka_peers(pb, ka, ka_size)
        signal_peers(over_pb + over_ka)
        out_ref[ka, pb] = x_ref[...]
        await_peers(len(over_pb) + len(over_ka))
        wait_all(run_all([
            push(x_ref, out_ref.at[ka, pb], pb_send.at[k], pb_recv.at[k], peer)
            for k, peer in enumerate(over_pb)
        ]))
        wait_all(run_all([
            push(out_ref.at[ka], out_ref.at[ka], ka_send.at[k], ka_recv.at[k], peer)
            for k, peer in enumerate(over_ka)
        ]))

    return small_call(
        body,
        jax.ShapeDtypeStruct((ka_size, pb_size) + bias.shape, bias.dtype),
        [dma((pb_size,)), dma((pb_size,)), dma((ka_size,)), dma((ka_size,))],
        0, "bias_gather", bias,
    )


def stats_exchange(stats, pb_size, ka_size):
    def body(x_ref, out_ref, slots, own, pb_send, pb_recv, ka_send, ka_recv):
        pb, ka = lax.axis_index("pb"), lax.axis_index("ka")
        over_pb, over_ka = pb_peers(pb, ka, pb_size), ka_peers(pb, ka, ka_size)
        signal_peers(over_pb + over_ka)
        slots[ka] = x_ref[...]
        await_peers(len(over_pb) + len(over_ka))
        wait_all(run_all([
            push(x_ref, slots.at[ka], ka_send.at[k], ka_recv.at[k], peer)
            for k, peer in enumerate(over_ka)
        ]))
        top = slots[0, 0:1, :]
        for k in range(1, ka_size):
            top = jnp.maximum(top, slots[k, 0:1, :])
        row_sum, dots = jnp.zeros_like(top), jnp.zeros_like(top)
        for k in range(ka_size):
            share = jnp.exp2(slots[k, 0:1, :] - top)
            row_sum = row_sum + slots[k, 1:2, :] * share
            dots = dots + slots[k, 2:3, :] * share
        joined = jnp.concatenate([top + jnp.log2(row_sum), dots / row_sum], axis=0)
        own[...] = joined
        out_ref[pb] = joined
        wait_all(run_all([
            push(own, out_ref.at[pb], pb_send.at[k], pb_recv.at[k], peer)
            for k, peer in enumerate(over_pb)
        ]))

    rows = stats.shape[1]
    return small_call(
        body,
        jax.ShapeDtypeStruct((pb_size, 2, rows), jnp.float32),
        [
            pltpu.VMEM((ka_size,) + stats.shape, jnp.float32),
            pltpu.VMEM((2, rows), jnp.float32),
            dma((pb_size,)), dma((pb_size,)), dma((ka_size,)), dma((ka_size,)),
        ],
        1, "stats_exchange", stats,
    )


def diagonal_reduce(spread):
    pb_size, ka_size = spread.shape[:2]

    def body(x_ref, out_ref, slots, part, got, pb_send, pb_recv, ka_send, ka_recv):
        pb, ka = lax.axis_index("pb"), lax.axis_index("ka")
        over_pb, over_ka = pb_peers(pb, ka, pb_size), ka_peers(pb, ka, ka_size)
        signal_peers(over_pb + over_ka)
        slots[ka] = x_ref[:, ka]
        await_peers(len(over_pb) + len(over_ka))
        wait_all(run_all([
            push(x_ref.at[:, peer[1]], slots.at[ka], ka_send.at[k], ka_recv.at[k], peer)
            for k, peer in enumerate(over_ka)
        ]))
        total = slots[0]
        for k in range(1, ka_size):
            total = total + slots[k]
        part[...] = total
        got[pb] = part[pb]
        wait_all(run_all([
            push(part.at[peer[0]], got.at[pb], pb_send.at[k], pb_recv.at[k], peer)
            for k, peer in enumerate(over_pb)
        ]))
        total = got[0]
        for k in range(1, pb_size):
            total = total + got[k]
        out_ref[...] = total

    block = spread.shape[2:]
    f32 = jnp.float32
    return small_call(
        body,
        jax.ShapeDtypeStruct(block, f32),
        [
            pltpu.VMEM((ka_size, pb_size) + block, f32),
            pltpu.VMEM((pb_size,) + block, f32),
            pltpu.VMEM((pb_size,) + block, f32),
            dma((pb_size,)), dma((pb_size,)), dma((ka_size,)), dma((ka_size,)),
        ],
        2, "diagonal_reduce", spread,
    )


def build_table(w_ref, t_ref, tiles):
    def one(t, carry):
        first = w_ref[pl.ds(tiles - 1 - t, 1), :]
        second = w_ref[pl.ds(tiles - t, 1), :]
        wide = jnp.broadcast_to(jnp.concatenate([first, second], axis=1), (LANES, 2 * LANES))
        turned = pltpu.roll(wide, LANES + 1, axis=1, stride=1, stride_axis=0)
        t_ref[pl.ds(pl.multiple_of(t * LANES, LANES), LANES), :] = turned[:, :LANES]
        return carry

    lax.fori_loop(0, tiles, one, 0)


def stage_of(k, steps, pb_size):
    return 0 if k == 0 else 1 + (k - 1) * (steps - 1) // max(pb_size - 1, 1)


def forward_kernel(
    key_rows, factor, steps, pb_size, ka_size,
    w_ref, q_ref, g_ref, k_ref, v_ref, rows_ref, out_ref, rows_out,
    t_ref, m_ref, l_ref, d_ref,
    own_sem, pb_send, pb_recv, y_send, y_recv, core_send, core_recv,
):
    step = pl.program_id(0)
    chunk = k_ref.shape[0]
    blocks = q_ref.shape[0] // LANES
    tiles = t_ref.shape[0] // LANES
    pb, ka = lax.axis_index("pb"), lax.axis_index("ka")
    y_size = ka_size // 2
    y, core = ka // 2, lax.rem(ka, 2)
    over_pb = pb_peers(pb, ka, pb_size)
    over_y = [(pb, lax.rem(y + j, y_size) * 2 + core) for j in range(1, y_size)]
    partner = (pb, y * 2 + 1 - core)
    peers = over_pb + over_y + [partner]

    own_copy = pltpu.make_async_copy(rows_ref, rows_out.at[core, y, pb], own_sem)
    pb_copies = [
        push(rows_ref, rows_out.at[core, y, pb], pb_send.at[k], pb_recv.at[k], peer)
        for k, peer in enumerate(over_pb)
    ]

    def slot_of(k):
        return lax.rem(pb + pb_size - k, pb_size)

    def y_copies(k):
        slot = slot_of(k)
        source = rows_ref if k == 0 else rows_out.at[core, y, slot]
        return [
            push(source, rows_out.at[core, y, slot], y_send.at[j, k], y_recv.at[j, k], peer)
            for j, peer in enumerate(over_y)
        ]

    def core_copy(k):
        here = rows_out.at[core, :, slot_of(k)]
        return push(here, here, core_send.at[k], core_recv.at[k], partner)

    def relay(k):
        if k == 0:
            own_copy.wait()
        for copy in y_copies(k):
            copy.wait_recv()
        core_copy(k).start()

    @pl.when(step == 0)
    def _():
        signal_peers(peers)
        own_copy.start()
        build_table(w_ref, t_ref, tiles)
        m_ref[...] = jnp.full_like(m_ref, FLOOR)
        l_ref[...] = jnp.zeros_like(l_ref)
        d_ref[...] = jnp.zeros_like(d_ref)
        await_peers(len(peers))
        run_all(pb_copies)
        run_all(y_copies(0))

    for s in range(1, steps):
        @pl.when(step == s)
        def _(s=s):
            for k in range(1, pb_size):
                if stage_of(k, steps, pb_size) == s:
                    pb_copies[k - 1].wait_recv()
                    run_all(y_copies(k))
            for k in range(pb_size):
                if stage_of(k, steps, pb_size) == s - 1:
                    relay(k)

    def one(kb, carry):
        at = pl.multiple_of(kb * key_rows, key_rows)
        scores = dot_nt(k_ref[pl.ds(at, key_rows), :], q_ref[...])
        dprobs = dot_nt(v_ref[pl.ds(at, key_rows), :], g_ref[...])
        for b in range(blocks):
            lanes = slice(b * LANES, (b + 1) * LANES)
            kappa = pl.multiple_of(step * chunk + at + LANES * (blocks - 1 - b), LANES)
            s = scores[:, lanes] * factor + t_ref[pl.ds(kappa, key_rows), :]
            s = s.reshape(key_rows // 8, 8, LANES)
            d = dprobs[:, lanes].reshape(key_rows // 8, 8, LANES)
            old = m_ref[:, lanes]
            new = jnp.maximum(old, jnp.max(s, axis=0))
            e = jnp.exp2(s - new[None])
            alpha = jnp.exp2(old - new)
            m_ref[:, lanes] = new
            l_ref[:, lanes] = l_ref[:, lanes] * alpha + jnp.sum(e, axis=0)
            d_ref[:, lanes] = d_ref[:, lanes] * alpha + jnp.sum(e * d, axis=0)
        return carry

    lax.fori_loop(0, chunk // key_rows, one, 0)

    @pl.when(step == pl.num_programs(0) - 1)
    def _():
        m = m_ref[...]
        top = jnp.max(m, axis=0, keepdims=True)
        share = jnp.exp2(m - top)
        out_ref[0:1, :] = top
        out_ref[1:2, :] = jnp.sum(l_ref[...] * share, axis=0, keepdims=True)
        out_ref[2:3, :] = jnp.sum(d_ref[...] * share, axis=0, keepdims=True)
        out_ref[3:4, :] = jnp.zeros_like(top)
        for k in range(pb_size):
            if stage_of(k, steps, pb_size) == steps - 1:
                relay(k)
        for copy in pb_copies:
            copy.wait_send()
        for k in range(pb_size):
            for copy in y_copies(k):
                copy.wait_send()
            core_copy(k).wait()


def forward(window, queries, grads, keys, values, own_rows, factor, pb_size, ka_size):
    rows, dim = queries.shape
    count = keys.shape[0]
    chunk = min(1024, count // 4)
    tiles = count // LANES + rows // LANES - 1
    whole = lambda i: (0, 0)
    return pl.pallas_call(
        lambda *refs: forward_kernel(
            min(256, chunk), factor, count // chunk, pb_size, ka_size, *refs
        ),
        out_shape=(
            jax.ShapeDtypeStruct((4, rows), jnp.float32),
            jax.ShapeDtypeStruct((2, ka_size // 2, pb_size) + own_rows.shape, own_rows.dtype),
        ),
        grid=(count // chunk,),
        in_specs=[
            pl.BlockSpec(window.shape, whole),
            pl.BlockSpec((rows, dim), whole),
            pl.BlockSpec((rows, dim), whole),
            pl.BlockSpec((chunk, dim), lambda i: (i, 0)),
            pl.BlockSpec((chunk, dim), lambda i: (i, 0)),
            pl.BlockSpec(memory_space=pl.ANY),
        ],
        out_specs=(pl.BlockSpec((4, rows), whole), pl.BlockSpec(memory_space=pl.ANY)),
        scratch_shapes=[
            pltpu.VMEM((tiles * LANES, LANES), jnp.float32),
            pltpu.VMEM((8, rows), jnp.float32),
            pltpu.VMEM((8, rows), jnp.float32),
            pltpu.VMEM((8, rows), jnp.float32),
            dma, dma((pb_size,)), dma((pb_size,)), dma((ka_size, pb_size)), dma((ka_size, pb_size)),
            dma((pb_size,)), dma((pb_size,)),
        ],
        compiler_params=pltpu.CompilerParams(collective_id=3, has_side_effects=True),
        name="forward",
    )(window, queries, grads, keys, values, own_rows)


def fold_diagonals(g_ref, diag_ref, tiles):
    diag_ref[...] = jnp.zeros_like(diag_ref)

    def one(t, carry):
        tile = g_ref[pl.ds(pl.multiple_of(t * LANES, LANES), LANES), :]
        x = jnp.concatenate([tile, jnp.zeros_like(tile)], axis=1)
        half = LANES // 2
        while half >= 8:
            x = pltpu.roll(x[:half], half, axis=1) + x[half:]
            half //= 2
        for part in (4, 2, 1):
            x = pltpu.roll(x, part, axis=1) + pltpu.roll(x, 8 - part, axis=0)
        low = pl.ds(tiles - 1 - t, 1)
        high = pl.ds(tiles - t, 1)
        diag_ref[low, :] = diag_ref[low, :] + x[0:1, :LANES]
        diag_ref[high, :] = diag_ref[high, :] + x[0:1, LANES:]
        return carry

    lax.fori_loop(0, tiles, one, 0)


def backward_kernel(
    key_rows, factor, scale, pb_size, ka_size,
    w_ref, rows_ref, stats_ref, k_ref, v_ref, kt_ref,
    dq_ref, dk_ref, dv_ref, diag_ref, t_ref, g_ref, dk_acc, dv_acc, dq_acc,
    dq_sent, dq_got, send_sems, recv_sems,
):
    step = pl.program_id(0)
    dim = k_ref.shape[1]
    chunk = stats_ref.shape[2]
    pb, ka = lax.axis_index("pb"), lax.axis_index("ka")
    turn = lax.rem(pb + 1 + step, pb_size)
    peers = []
    for i in range(pb_size):
        for j in range(ka_size):
            if (i, j) != (pb_size - 1, 0):
                peers.append((lax.rem(pb + 1 + i, pb_size), lax.rem(ka + j, ka_size)))
    here_id = pb * ka_size + ka

    def term_copy(i, j):
        target = lax.rem(ka + j, ka_size)
        return push(
            dq_sent.at[i, target], dq_got.at[here_id], send_sems.at[i, j], recv_sems.at[i, j],
            (lax.rem(pb + 1 + i, pb_size), target),
        )

    blocks = chunk // LANES
    tiles = t_ref.shape[0] // LANES
    last_block = tiles - k_ref.shape[0] // LANES

    @pl.when(step == 0)
    def _():
        signal_peers(peers)
        build_table(w_ref, t_ref, tiles)
        g_ref[...] = jnp.zeros_like(g_ref)
        dk_acc[...] = jnp.zeros_like(dk_acc)
        dv_acc[...] = jnp.zeros_like(dv_acc)

    @pl.when(step == 1)
    def _():
        await_peers(len(peers))

    @pl.when(step >= 1)
    def _():
        for j in range(ka_size):
            term_copy(step - 1, j).start()

    rows = jnp.concatenate([rows_ref[k % 2, k // 2, 0] for k in range(ka_size)], axis=0)
    lse_row, dots_row = stats_ref[0, 0:1, :], stats_ref[0, 1:2, :]
    q, g = rows[:, :dim], rows[:, dim:]
    dq_acc[...] = jnp.zeros_like(dq_acc)

    def one(kb, carry):
        at = pl.multiple_of(kb * key_rows, key_rows)
        here = pl.ds(at, key_rows)
        scores = dot_nt(k_ref[here, :], q)
        dprobs = dot_nt(v_ref[here, :], g)
        probs_low, dscores_low = [], []
        for b in range(blocks):
            lanes = slice(b * LANES, (b + 1) * LANES)
            kappa = pl.multiple_of(at + LANES * (last_block - turn * blocks - b), LANES)
            there = pl.ds(kappa, key_rows)
            s = scores[:, lanes] * factor + t_ref[there, :]
            p = jnp.exp2(s - lse_row[:, lanes])
            ds = p * (dprobs[:, lanes] - dots_row[:, lanes])
            g_ref[there, :] = g_ref[there, :] + ds
            probs_low.append(p.astype(jnp.bfloat16))
            dscores_low.append(ds.astype(jnp.bfloat16))
        p_low = jnp.concatenate(probs_low, axis=1)
        ds_low = jnp.concatenate(dscores_low, axis=1)
        dv_acc[here, :] += dot_nn(p_low, g)
        dk_acc[here, :] += dot_nn(ds_low, q)
        dq_acc[...] += dot_nn(kt_ref[kb], ds_low)
        return carry

    lax.fori_loop(0, k_ref.shape[0] // key_rows, one, 0)

    width = dq_sent.shape[3]
    for b in range(ka_size):
        dq_sent[step, b] = dq_acc[:, b * width : (b + 1) * width].astype(dq_sent.dtype)

    @pl.when(step == pb_size - 1)
    def _():
        dk_ref[...] = (dk_acc[...] * scale).astype(dk_ref.dtype)
        dv_ref[...] = dv_acc[...].astype(dv_ref.dtype)
        for j in range(1, ka_size):
            term_copy(pb_size - 1, j).start()
        dq_got[here_id] = dq_sent[pb_size - 1, ka]
        fold_diagonals(g_ref, diag_ref, tiles)
        for i in range(pb_size):
            for j in range(ka_size):
                if (i, j) != (pb_size - 1, 0):
                    term_copy(i, j).wait()
        total = dq_got[0].astype(jnp.float32)
        for k in range(1, pb_size * ka_size):
            total = total + dq_got[k].astype(jnp.float32)
        dq_ref[...] = (total.T * scale).astype(dq_ref.dtype)


def backward(window, rows, stats, keys, values, factor, scale):
    cores, y_size, pb_size, part_rows, wide = rows.shape
    ka_size = cores * y_size
    count, dim = keys.shape
    chunk = ka_size * part_rows
    tiles = count // LANES + pb_size * chunk // LANES - 1
    key_rows = min(256, count)
    keys_turned = keys.reshape(count // key_rows, key_rows, dim).swapaxes(1, 2)
    whole = lambda i: (0, 0)
    f32 = jnp.float32

    def turn(i):
        return lax.rem(lax.axis_index("pb") + 1 + i, pb_size)

    return pl.pallas_call(
        lambda *refs: backward_kernel(key_rows, factor, scale, pb_size, ka_size, *refs),
        out_shape=(
            jax.ShapeDtypeStruct((part_rows, dim), jnp.bfloat16),
            jax.ShapeDtypeStruct((count, dim), jnp.bfloat16),
            jax.ShapeDtypeStruct((count, dim), jnp.bfloat16),
            jax.ShapeDtypeStruct(window.shape, f32),
        ),
        grid=(pb_size,),
        in_specs=[
            pl.BlockSpec(window.shape, whole),
            pl.BlockSpec((cores, y_size, 1, part_rows, wide), lambda i: (0, 0, turn(i), 0, 0)),
            pl.BlockSpec((1, 2, chunk), lambda i: (turn(i), 0, 0)),
            pl.BlockSpec((count, dim), whole),
            pl.BlockSpec((count, dim), whole),
            pl.BlockSpec(keys_turned.shape, lambda i: (0, 0, 0)),
        ],
        out_specs=(
            pl.BlockSpec((part_rows, dim), whole),
            pl.BlockSpec((count, dim), whole),
            pl.BlockSpec((count, dim), whole),
            pl.BlockSpec(window.shape, whole),
        ),
        scratch_shapes=[
            pltpu.VMEM((tiles * LANES, LANES), f32),
            pltpu.VMEM((tiles * LANES, LANES), f32),
            pltpu.VMEM((count, dim), f32),
            pltpu.VMEM((count, dim), f32),
            pltpu.VMEM((dim, chunk), f32),
            pltpu.VMEM((pb_size, ka_size, dim, part_rows), jnp.bfloat16),
            pltpu.VMEM((pb_size * ka_size, dim, part_rows), jnp.bfloat16),
            dma((pb_size, ka_size)), dma((pb_size, ka_size)),
        ],
        compiler_params=pltpu.CompilerParams(collective_id=4, has_side_effects=True),
        name="backward",
    )(window, rows, stats, keys, values, keys_turned)


def on_device(queries, keys, values, bias, grad_out, group_start):
    pb_size, ka_size = lax.axis_size("pb"), lax.axis_size("ka")
    pb, ka = lax.axis_index("pb"), lax.axis_index("ka")
    rows, dim = queries.shape
    key_count = keys.shape[0]
    total_rows = rows * pb_size
    scale = dim ** (-0.5)
    factor = scale * LOG2E
    first = group_start[0]

    part_rows = rows // ka_size
    both = jnp.concatenate([queries, grad_out], axis=1)
    own_rows = lax.dynamic_slice_in_dim(both, ka * part_rows, part_rows, 0)
    bias_all = bias_gather(bias.reshape(-1, LANES), pb_size, ka_size).swapaxes(0, 1)

    bias_count = bias.shape[0] * pb_size * ka_size
    margin = key_count * ka_size
    tail = 2 * LANES
    table = jnp.concatenate(
        [
            jnp.full((margin,), NEGATIVE, jnp.float32),
            bias_all.reshape(-1) * LOG2E,
            jnp.zeros((tail,), jnp.float32),
        ]
    )

    def window_of(query_first, key_first, query_rows, key_rows):
        low = query_first - key_first - key_rows + 1 + margin
        size = key_rows + query_rows
        return low, lax.dynamic_slice_in_dim(table, low, size).reshape(-1, LANES)

    key_base = ka * key_count
    low, window = window_of(first + pb * rows, key_base, rows, key_count)
    stats, row_all = forward(
        window, queries, grad_out, keys, values, own_rows, factor, pb_size, ka_size
    )
    stats = stats_exchange(stats, pb_size, ka_size)

    own_count = key_count // pb_size
    own_keys = lax.dynamic_slice_in_dim(keys, pb * own_count, own_count, 0)
    own_values = lax.dynamic_slice_in_dim(values, pb * own_count, own_count, 0)
    low, window = window_of(first, key_base + pb * own_count, total_rows, own_count)
    query_grad, key_grad, value_grad, diag = backward(
        window, row_all, stats, own_keys, own_values, factor, scale
    )
    spread = lax.dynamic_update_slice_in_dim(
        jnp.zeros(table.shape, jnp.float32), diag.reshape(-1), low, 0
    )
    spread = spread[margin : margin + bias_count].reshape(pb_size, ka_size, -1, LANES)
    bias_grad = diagonal_reduce(spread)
    return query_grad, key_grad, value_grad, bias_grad.reshape(-1)


def solution(mesh):
    return jax.shard_map(
        on_device,
        mesh=mesh,
        in_specs=(P("pb", None), P("ka", None), P("ka", None), P(("pb", "ka")), P("pb", None), P()),
        out_specs=(
            P(("pb", "ka"), None),
            P(("ka", "pb"), None),
            P(("ka", "pb"), None),
            P(("pb", "ka")),
        ),
        check_vma=False,
    )
```

time: 167 us -> 133 us (0.80)
  Pallas kernels: 147 us -> 117 us
  local copies, waits for them, and re-layouts: 15 us -> 11.6 us
    pallas_call x5, Pallas kernels: 147 us -> 117 us  [the longest x1 44.3 us: backward(): pl.pallas_call(lambda *refs: backward_kernel(key_rows, factor, scale, pb_...]
    transpose x1 -> x0, local copies, waits for them, and re-layouts: 3.16 us -> none  [on_device(): row_all.swapaxes(0, 1).reshape(ka_size, pb_size, part_rows, 2 * dim)]
    reshape x3 -> x0, local copies, waits for them, and re-layouts: 2.98 us -> none  [the longest x1 1.3 us: on_device(): stats_all = gather_small(stats.reshape(-1, LANES), pb_size, ka_size, 1)]
    unnamed x6, local copies, waits for them, and re-layouts: 3.87 us -> 5.98 us
where the time goes in v2:
time: 133 us; the launch traced here: 132 us
  Pallas kernels  117 us (88%)
  local copies, waits for them, and re-layouts  11.6 us (9%)
  other arithmetic  2.35 us (2%)
  between operations  1.4 us (1%)
    pallas_call x1, Pallas kernels, backward(): pl.pallas_call(lambda *refs: backward_kernel(key_rows, factor, scale, pb_...  44.3 us
    pallas_call x1, Pallas kernels, forward(): pl.pallas_call(lambda *refs: forward_kernel(min(256, chunk), factor, coun...  37.6 us
    pallas_call x3, Pallas kernels, small_call(): pl.pallas_call(body, out_shape=out_shape, in_specs=[VMEM] * len(operands)...  35.2 us
    unnamed x6, local copies, waits for them, and re-layouts  5.98 us

profile of v2, /device:TPU:0, one launch (start us, length us, event | category | flops | bytes accessed | tf_op | source)
XLA Modules:
  0.0 132.4 jit_solution(18348230639372197712)
XLA Ops:
  1.3 13.3 %bias_gather.1 = f32[4,8,8,128]{3,2,1,0:T(8,128)} custom-call(f32[8,128]{1,0:T(8,128)} %bitcast.22), custom_call_target="tpu_custom_call" | custom-call | tf_op jit(solution)/shard_map/bias_gather/pallas_call | solution.py:66
  14.6 0.9 multiply_bitcast_fusion
  15.6 0.7 dynamic-slice_bitcast_fusion.refs_0_
  16.3 1.4 %fusion.refs_5_ = bf16[128,256]{1,0:T(8,128)(2,1)} fusion(s32[]{:T(128)S(6)} %select_n.16, bf16[512,128]{1,0:T(8,128)(2,1)} %refs_1_.1, bf16[512,128]{1,0:T(8,128)(2,1)} %refs_2_.1), kind=kLoop, calls=%fused_computation.4 | loop fusion | flops 131072 | bytes 327684 | tf_op jit(solution)/shard_map/concatenate | solution.py:528
  17.7 37.6 %forward.1 = (f32[4,512]{1,0:T(4,128)}, bf16[2,2,8,128,256]{4,3,2,1,0:T(8,128)(2,1)}) custom-call(f32[68,128]{1,0:T(8,128)} %dynamic-slice_bitcast_fusion.refs_0_, bf16[512,128]{1,0:T(8,128)(2,1)} %refs_1_.1, bf16[512,128]{1,0:T(8,128)(2,1)} %refs_2_.1, bf16[8192,128]{1,0:T(8,128)(2,1)} %refs_3_.1, bf16[8192,128]{1,0:T(8,128)(2,1)} %refs_4_.1, ...), custom_call_target="tpu_custom_call" | custom-call | tf_op jit(solution)/shard_map/forward/pallas_call | solution.py:315
  55.3 11.2 %stats_exchange.1.refs_2_ = f32[8,2,512]{2,1,0:T(2,128)} custom-call(f32[4,512]{1,0:T(4,128)} %get-tuple-element.11.x_ref), custom_call_target="tpu_custom_call" | custom-call | tf_op jit(solution)/shard_map/stats_exchange/pallas_call | solution.py:66
  66.5 0.7 dynamic-slice_bitcast_fusion.1.refs_0_
  67.2 1.8 %constant_dynamic-slice_fusion = (bf16[1024,128]{1,0:T(8,128)(2,1)}, bf16[1024,128]{1,0:T(8,128)(2,1)S(1)}) fusion(bf16[8192,128]{1,0:T(8,128)(2,1)} %refs_4_.1, s32[]{:T(128)S(6)} %select_n.17, bf16[8192,128]{1,0:T(8,128)(2,1)} %refs_3_.1), kind=kLoop, calls=%fused_computation.8 | loop fusion | bytes 1048580 | tf_op jit(solution)/shard_map/dynamic_slice | solution.py:557
  69.0 0.0 copy-start
  69.0 0.8 copy.11
  69.8 0.0 copy-done
  69.8 44.3 %backward.1 = (bf16[128,128]{1,0:T(8,128)(2,1)}, bf16[1024,128]{1,0:T(8,128)(2,1)}, bf16[1024,128]{1,0:T(8,128)(2,1)}, f32[40,128]{1,0:T(8,128)}) custom-call(f32[40,128]{1,0:T(8,128)} %dynamic-slice_bitcast_fusion.1.refs_0_, bf16[2,2,8,128,256]{4,3,2,1,0:T(8,128)(2,1)} %get-tuple-element.10.refs_1_, f32[8,2,512]{2,1,0:T(2,128)} %stats_exchange.1.refs_2_, ...), custom_call_target="tpu_custom_call" | custom-call | tf_op jit(solution)/shard_map/backward/pallas_call | solution.py:479
  114.2 0.9 bitcast_dynamic-update-slice_fusion
  115.1 0.7 slice.4
  115.7 10.7 %diagonal_reduce.1 = f32[8,128]{1,0:T(8,128)} custom-call(f32[8,4,8,128]{3,2,1,0:T(8,128)} %bitcast.19), custom_call_target="tpu_custom_call" | custom-call | tf_op jit(solution)/shard_map/diagonal_reduce/pallas_call | solution.py:66
  126.4 1.4 %copy.18 = bf16[128,128]{1,0:T(8,128)(2,1)} copy(bf16[128,128]{1,0:T(8,128)(2,1)} %get-tuple-element.22) | data formatting | bytes 65536
  127.8 1.7 %copy.19 = bf16[1024,128]{1,0:T(8,128)(2,1)} copy(bf16[1024,128]{1,0:T(8,128)(2,1)} %get-tuple-element.23) | data formatting | bytes 524288
  129.5 1.7 %copy.20 = bf16[1024,128]{1,0:T(8,128)(2,1)} copy(bf16[1024,128]{1,0:T(8,128)(2,1)} %get-tuple-element.24) | data formatting | bytes 524288
  131.1 1.3 copy.21
  (5 shorter events, 0.1 us)
Async XLA Ops:
  69.0 0.8 copy-start

commit v3 on v2

--- a/solution.py
+++ b/solution.py
@@ -67,74 +67,48 @@
         body,
         out_shape=out_shape,
         in_specs=[VMEM] * len(operands),
-        out_specs=VMEM,
+        out_specs=jax.tree.map(lambda leaf: VMEM, out_shape),
         scratch_shapes=scratch,
         compiler_params=pltpu.CompilerParams(collective_id=collective_id, has_side_effects=True),
         name=name,
     )(*operands)
 
 
-def bias_gather(bias, pb_size, ka_size):
-    def body(x_ref, out_ref, pb_send, pb_recv, ka_send, ka_recv):
+def entry_gather(bias, rows, pb_size, ka_size):
+    def body(
+        x_ref, rows_ref, out_ref, rows_out,
+        pb_send, pb_recv, ka_send, ka_recv, rows_send, rows_recv,
+    ):
         pb, ka = lax.axis_index("pb"), lax.axis_index("ka")
         over_pb, over_ka = pb_peers(pb, ka, pb_size), ka_peers(pb, ka, ka_size)
         signal_peers(over_pb + over_ka)
         out_ref[ka, pb] = x_ref[...]
         await_peers(len(over_pb) + len(over_ka))
-        wait_all(run_all([
+        first = run_all([
             push(x_ref, out_ref.at[ka, pb], pb_send.at[k], pb_recv.at[k], peer)
             for k, peer in enumerate(over_pb)
-        ]))
+        ])
+        rows_copies = run_all([
+            push(rows_ref, rows_out.at[pb], rows_send.at[k], rows_recv.at[k], peer)
+            for k, peer in enumerate(over_pb)
+        ])
+        rows_out[pb] = rows_ref[...]
+        wait_all(first)
         wait_all(run_all([
             push(out_ref.at[ka], out_ref.at[ka], ka_send.at[k], ka_recv.at[k], peer)
             for k, peer in enumerate(over_ka)
         ]))
+        wait_all(rows_copies)
 
     return small_call(
         body,
-        jax.ShapeDtypeStruct((ka_size, pb_size) + bias.shape, bias.dtype),
-        [dma((pb_size,)), dma((pb_size,)), dma((ka_size,)), dma((ka_size,))],
-        0, "bias_gather", bias,
-    )
-
-
-def stats_exchange(stats, pb_size, ka_size):
-    def body(x_ref, out_ref, slots, own, pb_send, pb_recv, ka_send, ka_recv):
-        pb, ka = lax.axis_index("pb"), lax.axis_index("ka")
-        over_pb, over_ka = pb_peers(pb, ka, pb_size), ka_peers(pb, ka, ka_size)
-        signal_peers(over_pb + over_ka)
-        slots[ka] = x_ref[...]
-        await_peers(len(over_pb) + len(over_ka))
-        wait_all(run_all([
-            push(x_ref, slots.at[ka], ka_send.at[k], ka_recv.at[k], peer)
-            for k, peer in enumerate(over_ka)
-        ]))
-        top = slots[0, 0:1, :]
-        for k in range(1, ka_size):
-            top = jnp.maximum(top, slots[k, 0:1, :])
-        row_sum, dots = jnp.zeros_like(top), jnp.zeros_like(top)
-        for k in range(ka_size):
-            share = jnp.exp2(slots[k, 0:1, :] - top)
-            row_sum = row_sum + slots[k, 1:2, :] * share
-            dots = dots + slots[k, 2:3, :] * share
-        joined = jnp.concatenate([top + jnp.log2(row_sum), dots / row_sum], axis=0)
-        own[...] = joined
-        out_ref[pb] = joined
-        wait_all(run_all([
-            push(own, out_ref.at[pb], pb_send.at[k], pb_recv.at[k], peer)
-            for k, peer in enumerate(over_pb)
-        ]))
-
-    rows = stats.shape[1]
-    return small_call(
-        body,
-        jax.ShapeDtypeStruct((pb_size, 2, rows), jnp.float32),
-        [
-            pltpu.VMEM((ka_size,) + stats.shape, jnp.float32),
-            pltpu.VMEM((2, rows), jnp.float32),
-            dma((pb_size,)), dma((pb_size,)), dma((ka_size,)), dma((ka_size,)),
-        ],
-        1, "stats_exchange", stats,
+        (
+            jax.ShapeDtypeStruct((ka_size, pb_size) + bias.shape, bias.dtype),
+            jax.ShapeDtypeStruct((pb_size,) + rows.shape, rows.dtype),
+        ),
+        [dma((pb_size,)), dma((pb_size,)), dma((ka_size,)), dma((ka_size,)),
+         dma((pb_size,)), dma((pb_size,))],
+        0, "entry_gather", bias, rows,
     )
 
 
@@ -192,15 +166,11 @@
     lax.fori_loop(0, tiles, one, 0)
 
 
-def stage_of(k, steps, pb_size):
-    return 0 if k == 0 else 1 + (k - 1) * (steps - 1) // max(pb_size - 1, 1)
-
-
 def forward_kernel(
     key_rows, factor, steps, pb_size, ka_size,
     w_ref, q_ref, g_ref, k_ref, v_ref, rows_ref, out_ref, rows_out,
     t_ref, m_ref, l_ref, d_ref,
-    own_sem, pb_send, pb_recv, y_send, y_recv, core_send, core_recv,
+    slots, joined, own_sem, y_send, y_recv, core_send, core_recv, ka_send, ka_recv, pb_send, pb_recv,
 ):
     step = pl.program_id(0)
     chunk = k_ref.shape[0]
@@ -212,35 +182,20 @@
     over_pb = pb_peers(pb, ka, pb_size)
     over_y = [(pb, lax.rem(y + j, y_size) * 2 + core) for j in range(1, y_size)]
     partner = (pb, y * 2 + 1 - core)
-    peers = over_pb + over_y + [partner]
-
-    own_copy = pltpu.make_async_copy(rows_ref, rows_out.at[core, y, pb], own_sem)
-    pb_copies = [
-        push(rows_ref, rows_out.at[core, y, pb], pb_send.at[k], pb_recv.at[k], peer)
-        for k, peer in enumerate(over_pb)
+    over_ka = ka_peers(pb, ka, ka_size)
+    peers = over_pb + over_ka
+
+    own_copy = pltpu.make_async_copy(rows_ref, rows_out.at[core, y], own_sem)
+    y_copies = [
+        push(rows_ref, rows_out.at[core, y], y_send.at[j], y_recv.at[j], peer)
+        for j, peer in enumerate(over_y)
     ]
 
-    def slot_of(k):
-        return lax.rem(pb + pb_size - k, pb_size)
-
-    def y_copies(k):
-        slot = slot_of(k)
-        source = rows_ref if k == 0 else rows_out.at[core, y, slot]
-        return [
-            push(source, rows_out.at[core, y, slot], y_send.at[j, k], y_recv.at[j, k], peer)
-            for j, peer in enumerate(over_y)
-        ]
-
-    def core_copy(k):
-        here = rows_out.at[core, :, slot_of(k)]
-        return push(here, here, core_send.at[k], core_recv.at[k], partner)
-
-    def relay(k):
-        if k == 0:
-            own_copy.wait()
-        for copy in y_copies(k):
-            copy.wait_recv()
-        core_copy(k).start()
+    def core_copy(j):
+        source = rows_out.at[core, lax.rem(y + y_size - j, y_size)]
+        return push(
+            rows_ref if j == 0 else source, source, core_send.at[j], core_recv.at[j], partner
+        )
 
     @pl.when(step == 0)
     def _():
@@ -251,22 +206,17 @@
         l_ref[...] = jnp.zeros_like(l_ref)
         d_ref[...] = jnp.zeros_like(d_ref)
         await_peers(len(peers))
-        run_all(pb_copies)
-        run_all(y_copies(0))
-
-    for s in range(1, steps):
-        @pl.when(step == s)
-        def _(s=s):
-            for k in range(1, pb_size):
-                if stage_of(k, steps, pb_size) == s:
-                    pb_copies[k - 1].wait_recv()
-                    run_all(y_copies(k))
-            for k in range(pb_size):
-                if stage_of(k, steps, pb_size) == s - 1:
-                    relay(k)
+        run_all(y_copies)
+        core_copy(0).start()
+
+    @pl.when(step == steps * 3 // 4)
+    def _():
+        for j, copy in enumerate(y_copies):
+            copy.wait_recv()
+            core_copy(j + 1).start()
 
     def one(kb, carry):
-        at = pl.multiple_of(kb * key_rows, key_rows)
+        at = kb * key_rows
         scores = dot_nt(k_ref[pl.ds(at, key_rows), :], q_ref[...])
         dprobs = dot_nt(v_ref[pl.ds(at, key_rows), :], g_ref[...])
         for b in range(blocks):
@@ -284,26 +234,42 @@
             d_ref[:, lanes] = d_ref[:, lanes] * alpha + jnp.sum(e * d, axis=0)
         return carry
 
-    lax.fori_loop(0, chunk // key_rows, one, 0)
+    for kb in range(chunk // key_rows):
+        one(kb, 0)
 
     @pl.when(step == pl.num_programs(0) - 1)
     def _():
         m = m_ref[...]
         top = jnp.max(m, axis=0, keepdims=True)
         share = jnp.exp2(m - top)
-        out_ref[0:1, :] = top
-        out_ref[1:2, :] = jnp.sum(l_ref[...] * share, axis=0, keepdims=True)
-        out_ref[2:3, :] = jnp.sum(d_ref[...] * share, axis=0, keepdims=True)
-        out_ref[3:4, :] = jnp.zeros_like(top)
-        for k in range(pb_size):
-            if stage_of(k, steps, pb_size) == steps - 1:
-                relay(k)
-        for copy in pb_copies:
+        slots[ka, 0:1, :] = top
+        slots[ka, 1:2, :] = jnp.sum(l_ref[...] * share, axis=0, keepdims=True)
+        slots[ka, 2:3, :] = jnp.sum(d_ref[...] * share, axis=0, keepdims=True)
+        slots[ka, 3:4, :] = jnp.zeros_like(top)
+        stat_copies = run_all([
+            push(slots.at[ka], slots.at[ka], ka_send.at[k], ka_recv.at[k], peer)
+            for k, peer in enumerate(over_ka)
+        ])
+        own_copy.wait()
+        for copy in y_copies:
             copy.wait_send()
-        for k in range(pb_size):
-            for copy in y_copies(k):
-                copy.wait_send()
-            core_copy(k).wait()
+        for j in range(y_size):
+            core_copy(j).wait()
+        wait_all(stat_copies)
+        best = slots[0, 0:1, :]
+        for k in range(1, ka_size):
+            best = jnp.maximum(best, slots[k, 0:1, :])
+        row_sum, dots = jnp.zeros_like(best), jnp.zeros_like(best)
+        for k in range(ka_size):
+            weight = jnp.exp2(slots[k, 0:1, :] - best)
+            row_sum = row_sum + slots[k, 1:2, :] * weight
+            dots = dots + slots[k, 2:3, :] * weight
+        joined[pb] = jnp.concatenate([best + jnp.log2(row_sum), dots / row_sum], axis=0)
+        wait_all(run_all([
+            push(joined.at[pb], joined.at[pb], pb_send.at[k], pb_recv.at[k], peer)
+            for k, peer in enumerate(over_pb)
+        ]))
+        out_ref[...] = joined[...]
 
 
 def forward(window, queries, grads, keys, values, own_rows, factor, pb_size, ka_size):
@@ -317,8 +283,8 @@
             min(256, chunk), factor, count // chunk, pb_size, ka_size, *refs
         ),
         out_shape=(
-            jax.ShapeDtypeStruct((4, rows), jnp.float32),
-            jax.ShapeDtypeStruct((2, ka_size // 2, pb_size) + own_rows.shape, own_rows.dtype),
+            jax.ShapeDtypeStruct((pb_size, 2, rows), jnp.float32),
+            jax.ShapeDtypeStruct((2, ka_size // 2) + own_rows.shape, own_rows.dtype),
         ),
         grid=(count // chunk,),
         in_specs=[
@@ -327,16 +293,18 @@
             pl.BlockSpec((rows, dim), whole),
             pl.BlockSpec((chunk, dim), lambda i: (i, 0)),
             pl.BlockSpec((chunk, dim), lambda i: (i, 0)),
-            pl.BlockSpec(memory_space=pl.ANY),
+            VMEM,
         ],
-        out_specs=(pl.BlockSpec((4, rows), whole), pl.BlockSpec(memory_space=pl.ANY)),
+        out_specs=(VMEM, pl.BlockSpec(memory_space=pl.ANY)),
         scratch_shapes=[
             pltpu.VMEM((tiles * LANES, LANES), jnp.float32),
             pltpu.VMEM((8, rows), jnp.float32),
             pltpu.VMEM((8, rows), jnp.float32),
             pltpu.VMEM((8, rows), jnp.float32),
-            dma, dma((pb_size,)), dma((pb_size,)), dma((ka_size, pb_size)), dma((ka_size, pb_size)),
-            dma((pb_size,)), dma((pb_size,)),
+            pltpu.VMEM((ka_size, 4, rows), jnp.float32),
+            pltpu.VMEM((pb_size, 2, rows), jnp.float32),
+            dma, dma((ka_size,)), dma((ka_size,)), dma((ka_size,)), dma((ka_size,)),
+            dma((ka_size,)), dma((ka_size,)), dma((pb_size,)), dma((pb_size,)),
         ],
         compiler_params=pltpu.CompilerParams(collective_id=3, has_side_effects=True),
         name="forward",
@@ -366,9 +334,9 @@
 
 def backward_kernel(
     key_rows, factor, scale, pb_size, ka_size,
-    w_ref, rows_ref, stats_ref, k_ref, v_ref, kt_ref,
+    w_ref, rows_ref, stats_ref, k_ref, v_ref,
     dq_ref, dk_ref, dv_ref, diag_ref, t_ref, g_ref, dk_acc, dv_acc, dq_acc,
-    dq_sent, dq_got, send_sems, recv_sems,
+    dq_sent, dq_got, kt_ref, send_sems, recv_sems,
 ):
     step = pl.program_id(0)
     dim = k_ref.shape[1]
@@ -398,6 +366,8 @@
         signal_peers(peers)
         build_table(w_ref, t_ref, tiles)
         g_ref[...] = jnp.zeros_like(g_ref)
+        for kb in range(k_ref.shape[0] // key_rows):
+            kt_ref[kb] = k_ref[kb * key_rows : (kb + 1) * key_rows, :].T
         dk_acc[...] = jnp.zeros_like(dk_acc)
         dv_acc[...] = jnp.zeros_like(dv_acc)
 
@@ -416,7 +386,7 @@
     dq_acc[...] = jnp.zeros_like(dq_acc)
 
     def one(kb, carry):
-        at = pl.multiple_of(kb * key_rows, key_rows)
+        at = kb * key_rows
         here = pl.ds(at, key_rows)
         scores = dot_nt(k_ref[here, :], q)
         dprobs = dot_nt(v_ref[here, :], g)
@@ -438,7 +408,8 @@
         dq_acc[...] += dot_nn(kt_ref[kb], ds_low)
         return carry
 
-    lax.fori_loop(0, k_ref.shape[0] // key_rows, one, 0)
+    for kb in range(k_ref.shape[0] // key_rows):
+        one(kb, 0)
 
     width = dq_sent.shape[3]
     for b in range(ka_size):
@@ -465,11 +436,10 @@
 def backward(window, rows, stats, keys, values, factor, scale):
     cores, y_size, pb_size, part_rows, wide = rows.shape
     ka_size = cores * y_size
-    count, dim = keys.shape
+    count, dim = keys.shape[0] // pb_size, keys.shape[1]
     chunk = ka_size * part_rows
     tiles = count // LANES + pb_size * chunk // LANES - 1
     key_rows = min(256, count)
-    keys_turned = keys.reshape(count // key_rows, key_rows, dim).swapaxes(1, 2)
     whole = lambda i: (0, 0)
     f32 = jnp.float32
 
@@ -489,9 +459,8 @@
             pl.BlockSpec(window.shape, whole),
             pl.BlockSpec((cores, y_size, 1, part_rows, wide), lambda i: (0, 0, turn(i), 0, 0)),
             pl.BlockSpec((1, 2, chunk), lambda i: (turn(i), 0, 0)),
-            pl.BlockSpec((count, dim), whole),
-            pl.BlockSpec((count, dim), whole),
-            pl.BlockSpec(keys_turned.shape, lambda i: (0, 0, 0)),
+            pl.BlockSpec((count, dim), lambda i: (lax.axis_index("pb"), 0)),
+            pl.BlockSpec((count, dim), lambda i: (lax.axis_index("pb"), 0)),
         ],
         out_specs=(
             pl.BlockSpec((part_rows, dim), whole),
@@ -507,11 +476,26 @@
             pltpu.VMEM((dim, chunk), f32),
             pltpu.VMEM((pb_size, ka_size, dim, part_rows), jnp.bfloat16),
             pltpu.VMEM((pb_size * ka_size, dim, part_rows), jnp.bfloat16),
+            pltpu.VMEM((count // key_rows, dim, key_rows), jnp.bfloat16),
             dma((pb_size, ka_size)), dma((pb_size, ka_size)),
         ],
         compiler_params=pltpu.CompilerParams(collective_id=4, has_side_effects=True),
         name="backward",
-    )(window, rows, stats, keys, values, keys_turned)
+    )(window, rows, stats, keys, values)
+
+
+def hand_over(*arrays):
+    def body(*refs):
+        for source, target in zip(refs[: len(arrays)], refs[len(arrays) :]):
+            target[...] = source[...]
+
+    return pl.pallas_call(
+        body,
+        out_shape=tuple(jax.ShapeDtypeStruct(x.shape, x.dtype) for x in arrays),
+        in_specs=[VMEM] * len(arrays),
+        out_specs=tuple(VMEM for x in arrays),
+        name="hand_over",
+    )(*arrays)
 
 
 def on_device(queries, keys, values, bias, grad_out, group_start):
@@ -527,7 +511,8 @@
     part_rows = rows // ka_size
     both = jnp.concatenate([queries, grad_out], axis=1)
     own_rows = lax.dynamic_slice_in_dim(both, ka * part_rows, part_rows, 0)
-    bias_all = bias_gather(bias.reshape(-1, LANES), pb_size, ka_size).swapaxes(0, 1)
+    bias_all, pb_rows = entry_gather(bias.reshape(-1, LANES), own_rows, pb_size, ka_size)
+    bias_all = bias_all.swapaxes(0, 1)
 
     bias_count = bias.shape[0] * pb_size * ka_size
     margin = key_count * ka_size
@@ -548,22 +533,22 @@
     key_base = ka * key_count
     low, window = window_of(first + pb * rows, key_base, rows, key_count)
     stats, row_all = forward(
-        window, queries, grad_out, keys, values, own_rows, factor, pb_size, ka_size
-    )
-    stats = stats_exchange(stats, pb_size, ka_size)
+        window, queries, grad_out, keys, values, pb_rows, factor, pb_size, ka_size
+    )
 
     own_count = key_count // pb_size
-    own_keys = lax.dynamic_slice_in_dim(keys, pb * own_count, own_count, 0)
-    own_values = lax.dynamic_slice_in_dim(values, pb * own_count, own_count, 0)
     low, window = window_of(first, key_base + pb * own_count, total_rows, own_count)
     query_grad, key_grad, value_grad, diag = backward(
-        window, row_all, stats, own_keys, own_values, factor, scale
+        window, row_all, stats, keys, values, factor, scale
     )
     spread = lax.dynamic_update_slice_in_dim(
         jnp.zeros(table.shape, jnp.float32), diag.reshape(-1), low, 0
     )
     spread = spread[margin : margin + bias_count].reshape(pb_size, ka_size, -1, LANES)
     bias_grad = diagonal_reduce(spread)
+    query_grad, key_grad, value_grad, bias_grad = hand_over(
+        query_grad, key_grad, value_grad, bias_grad
+    )
     return query_grad, key_grad, value_grad, bias_grad.reshape(-1)
 
 

time: 133 us -> 112 us (0.84)
  Pallas kernels: 117 us -> 105 us
  local copies, waits for them, and re-layouts: 11.6 us -> 2.99 us
    unnamed x6 -> x0, local copies, waits for them, and re-layouts: 5.98 us -> none
    pallas_call x3 -> x2, Pallas kernels: 35.2 us -> 30 us  [small_call(): pl.pallas_call(body, out_shape=out_shape, in_specs=[VMEM] * len(operands)...]
    pallas_call x1, Pallas kernels: 37.6 us -> 32.7 us  [forward(): pl.pallas_call(lambda *refs: forward_kernel(min(256, chunk), factor, coun...]
    pallas_call x1, Pallas kernels: 44.3 us -> 40.2 us  [backward(): pl.pallas_call(lambda *refs: backward_kernel(key_rows, factor, scale, pb_...]
    pallas_call x0 -> x1, Pallas kernels: none -> 1.87 us  [hand_over(): pl.pallas_call(body, out_shape=tuple((jax.ShapeDtypeStruct(x.shape, x.dty...]
    dynamic_slice x1 -> x0, local copies, waits for them, and re-layouts: 1.77 us -> none  [on_device(): own_values = lax.dynamic_slice_in_dim(values, pb * own_count, own_count, 0)]
where the time goes in v3:
time: 112 us; the launch traced here: 111 us
  Pallas kernels  105 us (94%)
  local copies, waits for them, and re-layouts  2.99 us (3%)
  other arithmetic  2.36 us (2%)
  between operations  1.38 us (1%)
    pallas_call x1, Pallas kernels, backward(): pl.pallas_call(lambda *refs: backward_kernel(key_rows, factor, scale, pb_...  40.2 us
    pallas_call x1, Pallas kernels, forward(): pl.pallas_call(lambda *refs: forward_kernel(min(256, chunk), factor, coun...  32.7 us
    pallas_call x2, Pallas kernels, small_call(): pl.pallas_call(body, out_shape=out_shape, in_specs=[VMEM] * len(operands)...  30 us

profile of v3, /device:TPU:0, one launch (start us, length us, event | category | flops | bytes accessed | tf_op | source)
XLA Modules:
  0.0 111.5 jit_solution(9062145119131411568)
XLA Ops:
  0.6 1.4 %fusion.rows_ref = bf16[128,256]{1,0:T(8,128)(2,1)} fusion(s32[]{:T(128)S(6)} %select_n.10, bf16[512,128]{1,0:T(8,128)(2,1)} %refs_1_.1, bf16[512,128]{1,0:T(8,128)(2,1)} %refs_2_.1), kind=kLoop, calls=%fused_computation.4 | loop fusion | flops 131072 | bytes 327684 | tf_op jit(solution)/shard_map/concatenate | solution.py:512
  2.1 18.5 %entry_gather.1 = (f32[4,8,8,128]{3,2,1,0:T(8,128)}, bf16[8,128,256]{2,1,0:T(8,128)(2,1)}) custom-call(f32[8,128]{1,0:T(8,128)} %bitcast.17, bf16[128,256]{1,0:T(8,128)(2,1)} %fusion.rows_ref), custom_call_target="tpu_custom_call" | custom-call | tf_op jit(solution)/shard_map/entry_gather/pallas_call | solution.py:66
  20.6 0.9 multiply_bitcast_fusion
  22.2 0.7 dynamic-slice_bitcast_fusion.1.refs_0_
  22.9 0.7 dynamic-slice_bitcast_fusion.refs_0_
  23.6 32.7 %forward.1 = (f32[8,2,512]{2,1,0:T(2,128)}, bf16[2,2,8,128,256]{4,3,2,1,0:T(8,128)(2,1)}) custom-call(f32[68,128]{1,0:T(8,128)} %dynamic-slice_bitcast_fusion.refs_0_, bf16[512,128]{1,0:T(8,128)(2,1)} %refs_1_.1, bf16[512,128]{1,0:T(8,128)(2,1)} %refs_2_.1, bf16[8192,128]{1,0:T(8,128)(2,1)} %refs_3_.3, bf16[8192,128]{1,0:T(8,128)(2,1)} %refs_4_.3, ...), custom_call_target="tpu_custom_call" | custom-call | tf_op jit(solution)/shard_map/forward/pallas_call | solution.py:281
  56.4 40.2 %backward.1 = (bf16[128,128]{1,0:T(8,128)(2,1)}, bf16[1024,128]{1,0:T(8,128)(2,1)}, bf16[1024,128]{1,0:T(8,128)(2,1)}, f32[40,128]{1,0:T(8,128)}) custom-call(f32[40,128]{1,0:T(8,128)} %dynamic-slice_bitcast_fusion.1.refs_0_, bf16[2,2,8,128,256]{4,3,2,1,0:T(8,128)(2,1)} %get-tuple-element.18.refs_1_, f32[8,2,512]{2,1,0:T(2,128)} %get-tuple-element.19.refs_2_, ...), custom_call_target="tpu_custom_call" | custom-call | tf_op jit(solution)/shard_map/backward/pallas_call | solution.py:449
  96.6 0.9 bitcast_dynamic-update-slice_fusion
  97.5 0.7 slice.4
  98.2 11.5 %diagonal_reduce.1.refs_3_ = f32[8,128]{1,0:T(8,128)} custom-call(f32[8,4,8,128]{3,2,1,0:T(8,128)} %bitcast.15), custom_call_target="tpu_custom_call" | custom-call | tf_op jit(solution)/shard_map/diagonal_reduce/pallas_call | solution.py:66
  109.6 1.9 %hand_over.1 = (bf16[128,128]{1,0:T(8,128)(2,1)}, bf16[1024,128]{1,0:T(8,128)(2,1)}, bf16[1024,128]{1,0:T(8,128)(2,1)}, f32[8,128]{1,0:T(8,128)}) custom-call(bf16[128,128]{1,0:T(8,128)(2,1)} %get-tuple-element.20.refs_0_, bf16[1024,128]{1,0:T(8,128)(2,1)} %get-tuple-element.21.refs_1_, bf16[1024,128]{1,0:T(8,128)(2,1)} %get-tuple-element.22.refs_2_, ...), custom_call_target="tpu_custom_call" | custom-call | tf_op jit(solution)/shard_map/hand_over/pallas_call | solution.py:492
  (5 shorter events, 0.1 us)
